TPU v7x, 256 devices: a whole 4x4x8 slice. The times are simulated.
256 devices in a mesh: row: 8 (over y, x_hi), col: 32 (over z, x_lo, core).
Axes of the slice: x: 4 (x_hi: 2, x_lo: 2; x = x_hi * 2 + x_lo), y: 4, z: 8, core: 2. Of those that a mesh axis runs over, the one named last changes fastest.
Arguments:
- tokens: bfloat16 [256, 12288], P('col', 'row'), may hold values from -6 to 6
- cotangent: bfloat16 [256, 12288], P('col', 'row'), may hold values from -6 to 6
- w1_mask: int32 [96, 384], P('row', 'col'), may hold values from 0 to 1, as said below
- w1_blocks: bfloat16 [8, 32, 48, 128, 128], P('row', 'col'), may hold values from -0.109375 to 0.109375
- bias: bfloat16 [49152], P('col'), may hold values from -4 to 4
- w2_mask: int32 [384, 96], P('col', 'row'), may hold values from 0 to 1, as said below
- w2_blocks: bfloat16 [8, 32, 48, 128, 128], P('row', 'col'), may hold values from -0.0546875 to 0.0546875
Outputs:
- out: bfloat16 [256, 12288], P('col', 'row')
- tokens_grad: bfloat16 [256, 12288], P('col', 'row')
- w1_grad: float32 [8, 32, 48, 128, 128], P('row', 'col')
- w2_grad: float32 [8, 32, 48, 128, 128], P('row', 'col')
- bias_grad: float32 [49152], P('col')
Inputs may be any that keep to these rules, and one draw needn't show every extreme that they name: `w1_mask`: in every block row, each aligned group of 8 blocks along the columns holds exactly two ones. One device's tile of 12 x 12 blocks holds at most 48 ones, and in every draw some device's tile holds exactly 48. `w2_mask`: in every block row, each aligned group of 8 blocks along the columns holds exactly two ones. One device's tile of 12 x 12 blocks holds at most 48 ones, and in every draw some device's tile holds exactly 48.
All inputs are finite; a program needn't handle non-finite values.
Results may differ from a plain program's by a relative error of at most 0.005.
Values may be sent and summed in bfloat16 or wider, within the bound.
A program may use at most 64 MiB of HBM per device.

v0:
```python
import math

import jax
import jax.numpy as jnp
from jax import lax
from jax.sharding import PartitionSpec as P

BLK = 128


slope_const = math.sqrt(2.0 / math.pi)


def gelu_value(values):
    inner = slope_const * (values + 0.044715 * values * values * values)
    return 0.5 * values * (1.0 + jnp.tanh(inner))


def gelu_slope(values):
    inner = slope_const * (values + 0.044715 * values * values * values)
    tangent = jnp.tanh(inner)
    return 0.5 * (1.0 + tangent) + 0.5 * values * (1.0 - tangent * tangent) * slope_const * (
        1.0 + 3.0 * 0.044715 * values * values
    )


def slot_layout(mask_tile, capacity):
    col_count = mask_tile.shape[1]
    flat = mask_tile.reshape(-1)
    order = jnp.argsort(1 - flat, stable=True)[:capacity]
    live_slot = jnp.arange(capacity, dtype=jnp.int32) < jnp.sum(flat)
    return (order // col_count, order % col_count, live_slot)


def sparse_apply(inputs, blocks, source, target, live_slot, outputs, flipped):
    row_count = inputs.shape[0]
    block_width = blocks.shape[1]
    pieces = inputs.reshape(row_count, -1, block_width)
    picked = jnp.take(pieces, source, axis=1)
    pattern = "tkb,kcb->ktc" if flipped else "tkb,kbc->ktc"
    products = jnp.einsum(pattern, picked, blocks, preferred_element_type=jnp.float32)
    placement_table = (
        (target[:, None] == jnp.arange(outputs, dtype=jnp.int32)[None, :]) & live_slot[:, None]
    ).astype(jnp.float32)
    summed = jnp.einsum(
        "ktc,ko->toc",
        products,
        placement_table,
        precision=lax.Precision.HIGHEST,
        preferred_element_type=jnp.float32,
    )
    return summed.reshape(row_count, outputs * block_width)


def block_grads(left, right, left_index, right_index, live_slot):
    row_count = left.shape[0]
    block_width = BLK
    left_picked = jnp.take(left.reshape(row_count, -1, block_width), left_index, axis=1)
    right_picked = jnp.take(right.reshape(row_count, -1, block_width), right_index, axis=1)
    grads = jnp.einsum(
        "tkb,tkc->kbc", left_picked, right_picked, preferred_element_type=jnp.float32
    )
    return grads * live_slot[:, None, None].astype(jnp.float32)


def local(tokens, cotangent, w1_mask, w1_blocks, bias, w2_mask, w2_blocks):
    full_tokens, full_cotangent = (
        lax.all_gather(tokens, "col", axis=0, tiled=True),
        lax.all_gather(cotangent, "col", axis=0, tiled=True),
    )
    first_blocks = w1_blocks[0, 0]
    second_blocks = w2_blocks[0, 0]
    w1_rows, w1_cols, w1_live = slot_layout(w1_mask, first_blocks.shape[0])
    w2_rows, w2_cols, w2_live = slot_layout(w2_mask, second_blocks.shape[0])
    model_blocks = w1_mask.shape[0]
    hidden_blocks = w1_mask.shape[1]
    bias_wide = bias.astype(jnp.float32)
    rows_part = full_tokens
    hidden = (
        lax.psum_scatter(
            sparse_apply(rows_part, first_blocks, w1_rows, w1_cols, w1_live, hidden_blocks, False),
            "row",
            scatter_dimension=0,
            tiled=True,
        )
        + bias_wide
    )
    activated = lax.all_gather(gelu_value(hidden).astype(jnp.bfloat16), "row", axis=0, tiled=True)
    out_terms = sparse_apply(
        activated, second_blocks, w2_rows, w2_cols, w2_live, model_blocks, False
    )
    rows_part = full_cotangent
    grad_act = lax.psum_scatter(
        sparse_apply(rows_part, second_blocks, w2_cols, w2_rows, w2_live, hidden_blocks, True),
        "row",
        scatter_dimension=0,
        tiled=True,
    )
    grad_hidden = lax.all_gather(
        (grad_act * gelu_slope(hidden)).astype(jnp.bfloat16), "row", axis=0, tiled=True
    )
    w2_grad = block_grads(activated, full_cotangent, w2_rows, w2_cols, w2_live)
    w1_grad = block_grads(full_tokens, grad_hidden, w1_rows, w1_cols, w1_live)
    bias_grad = jnp.sum(grad_hidden, axis=0, dtype=jnp.float32)
    grad_terms = sparse_apply(
        grad_hidden, first_blocks, w1_cols, w1_rows, w1_live, model_blocks, True
    )
    mixed, input_grad = (
        lax.psum_scatter(out_terms, "col", scatter_dimension=0, tiled=True),
        lax.psum_scatter(grad_terms, "col", scatter_dimension=0, tiled=True),
    )
    return (
        mixed.astype(jnp.bfloat16),
        input_grad.astype(jnp.bfloat16),
        w1_grad[None, None],
        w2_grad[None, None],
        bias_grad,
    )


def solution(mesh):
    return jax.shard_map(
        local,
        mesh=mesh,
        in_specs=(
            P("col", "row"),
            P("col", "row"),
            P("row", "col"),
            P("row", "col", None, None, None),
            P("col"),
            P("col", "row"),
            P("row", "col", None, None, None),
        ),
        out_specs=(
            P("col", "row"),
            P("col", "row"),
            P("row", "col", None, None, None),
            P("row", "col", None, None, None),
            P("col"),
        ),
        check_vma=False,
    )
```

profile of v0, /device:TPU:1, one launch (start us, length us, event | category | flops | bytes accessed | tf_op | source)
XLA Modules:
  0.0 531.0 jit_solution(4605489774764066578)
XLA Ops:
  7.2 1.5 fusion.81
  8.7 0.6 iota_compare_fusion.4
  9.4 3.2 sort.32
  12.7 40.9 %all_gather.12 = bf16[256,1536]{1,0:T(8,128)(2,1)S(1)} all-gather(bf16[8,1536]{1,0:T(8,128)(2,1)} %param.9), channel_id=1, replica_groups=mesh['row'=8,'col'=32] {'col'}, dimensions={0}, use_global_device_ids=true | all-gather | bytes 811008 | tf_op jit(solution)/shard_map/all_gather | solution.py:68
  53.8 0.4 copy.49
  54.2 2.7 gather_fusion
  56.9 2.9 fusion.20
  59.8 7.0 %fusion.30 = f32[256,12,128]{2,1,0:T(8,128)} fusion(f32[48,256,128]{2,1,0:T(8,128)S(1)} %fusion.20, s32[48]{0:T(128)S(1)} %get-tuple-element.26, pred[48]{0:T(512)(128)(4,1)S(1)} %iota_compare_fusion.4), kind=kOutput, calls=%fused_computation.32 | convolution fusion | flops 226493568 | bytes 7864560 | tf_op jit(solution)/shard_map/ktc,ko->toc/dot_general | solution.py:45
  66.9 1.8 copy.51
  68.8 1.6 copy.72
  70.5 33.2 %all_gather.14 = bf16[256,1536]{1,0:T(8,128)(2,1)S(1)} all-gather(bf16[8,1536]{1,0:T(8,128)(2,1)S(1)} %copy-done.4), channel_id=1, replica_groups=mesh['row'=8,'col'=32] {'col'}, dimensions={0}, use_global_device_ids=true | all-gather | bytes 811008 | tf_op jit(solution)/shard_map/all_gather | solution.py:69
  104.0 0.4 copy.58
  104.4 3.2 sort.31
  107.6 2.7 gather_fusion.2
  110.3 0.6 iota_compare_fusion.5
  111.0 3.4 fusion.14
  114.4 7.0 %fusion.36 = f32[256,12,128]{2,1,0:T(8,128)} fusion(f32[48,256,128]{2,1,0:T(8,128)S(1)} %fusion.14, s32[48]{0:T(128)S(1)} %get-tuple-element.40, pred[48]{0:T(512)(128)(4,1)S(1)} %iota_compare_fusion.5), kind=kOutput, calls=%fused_computation.34 | convolution fusion | flops 226493568 | bytes 7864560 | tf_op jit(solution)/shard_map/ktc,ko->toc/dot_general | solution.py:45
  121.4 1.8 copy.60
  123.3 1.6 copy.76
  125.0 20.0 %reduce-scatter.13.cloned.1.call-done = f32[32,1536]{1,0:T(8,128)} async-done(((f32[256,1536]{1,0:T(8,128)}), f32[32,1536]{1,0:T(8,128)}) %reduce-scatter.13.cloned.1.call-update) | async-done | bytes 196624 | tf_op jit(solution)/shard_map/reduce_scatter | solution.py:80
  145.0 82.3 %reduce-scatter.17.cloned.1.call-done = f32[32,1536]{1,0:T(8,128)} async-done(((f32[256,1536]{1,0:T(8,128)}), f32[32,1536]{1,0:T(8,128)}) %reduce-scatter.17.cloned.1.call-update) | async-done | bytes 196624 | tf_op jit(solution)/shard_map/reduce_scatter | solution.py:93
  227.3 1.2 fusion.52
  228.5 32.0 %all_gather.15 = bf16[256,1536]{1,0:T(8,128)(2,1)S(1)} all-gather(bf16[32,1536]{1,0:T(8,128)(2,1)S(1)} %get-tuple-element.33), channel_id=1, replica_groups=mesh['row'=8,'col'=32] {'row'}, dimensions={0}, use_global_device_ids=true | all-gather | bytes 884736 | tf_op jit(solution)/shard_map/all_gather | solution.py:99
  260.5 1.2 copy.62
  261.6 1.5 copy.63
  263.2 2.8 gather_fusion.3
  265.9 2.9 fusion.10
  268.8 7.0 %fusion.39 = f32[256,12,128]{2,1,0:T(8,128)} fusion(f32[48,256,128]{2,1,0:T(8,128)S(1)} %fusion.10, s32[48]{0:T(128)S(1)} %get-tuple-element.42, pred[48]{0:T(512)(128)(4,1)S(1)} %iota_compare_fusion.4), kind=kOutput, calls=%fused_computation.35 | convolution fusion | flops 226493568 | bytes 7864560 | tf_op jit(solution)/shard_map/ktc,ko->toc/dot_general | solution.py:45
  275.9 1.8 copy.65
  277.7 1.6 copy.78
  279.5 31.3 %all_gather.13 = bf16[256,1536]{1,0:T(8,128)(2,1)S(1)} all-gather(bf16[32,1536]{1,0:T(8,128)(2,1)S(1)} %get-tuple-element.34), channel_id=1, replica_groups=mesh['row'=8,'col'=32] {'row'}, dimensions={0}, use_global_device_ids=true | all-gather | bytes 884736 | tf_op jit(solution)/shard_map/all_gather | solution.py:88
  311.0 0.4 copy.54
  311.4 2.8 gather_fusion.1
  314.2 3.4 fusion.17
  317.5 7.0 %fusion.33 = f32[256,12,128]{2,1,0:T(8,128)} fusion(f32[48,256,128]{2,1,0:T(8,128)S(1)} %fusion.17, s32[48]{0:T(128)S(1)} %get-tuple-element.28, pred[48]{0:T(512)(128)(4,1)S(1)} %iota_compare_fusion.5), kind=kOutput, calls=%fused_computation.33 | convolution fusion | flops 226493568 | bytes 7864560 | tf_op jit(solution)/shard_map/ktc,ko->toc/dot_general | solution.py:45
  324.6 2.1 copy.56
  326.7 1.6 copy.74
  328.4 0.7 fusion.79
  329.0 0.7 fusion.80
  329.7 0.7 convert_reduce_fusion
  330.4 6.1 %multiply_bitcast_fusion = f32[1,1,48,128,128]{4,3,2,1,0:T(8,128)} fusion(f32[48]{0:T(128)S(1)} %fusion.79, bf16[48,256,128]{2,1,0:T(8,128)(2,1)} %gather_fusion.1, pred[48]{0:T(512)(128)(4,1)S(1)} %get-tuple-element.39, bf16[48,256,128]{2,1,0:T(8,128)(2,1)} %gather_fusion.2, pred[48]{0:T(512)(128)(4,1)S(1)} %get-tuple-element.27), kind=kOutput, calls=%fused_computation.26 | convolution fusion | flops 406585344 | bytes 9437472 | tf_op jit(solution)/shard_map/tkb,tkc->kbc/dot_general | solution.py:60
  336.5 3.1 multiply_bitcast_fusion.1
  339.6 62.6 %reduce-scatter.19.cloned.1.call-done = f32[8,1536]{1,0:T(8,128)} async-done(((f32[256,1536]{1,0:T(8,128)}), f32[8,1536]{1,0:T(8,128)}) %reduce-scatter.19.cloned.1.call-update) | async-done | bytes 49168
  402.2 1.0 copy.79
  403.2 0.8 copy.69
  404.0 118.2 %reduce-scatter.15.cloned.1.call-done = f32[8,1536]{1,0:T(8,128)} async-done(((f32[256,1536]{1,0:T(8,128)}), f32[8,1536]{1,0:T(8,128)}) %reduce-scatter.15.cloned.1.call-update) | async-done | bytes 49168
  522.2 1.0 copy.75
  523.2 0.8 copy.68
  (38 shorter events, 1.3 us)
Async XLA Ops:
  7.2 49.7 %copy-start = (bf16[1,1,48,128,128]{4,3,2,1,0:T(8,128)(2,1)S(1)}, bf16[1,1,48,128,128]{4,3,2,1,0:T(8,128)(2,1)}, u32[]{:S(2)}) copy-start(bf16[1,1,48,128,128]{4,3,2,1,0:T(8,128)(2,1)} %param.12) | copy-start | bytes 4718596
  7.2 137.8 %reduce-scatter.13.cloned.1.call-start = ((), (), s32[]{:S(2)}) async-start(), calls=%async_computation.4 | async-start | bytes 1769472 | tf_op jit(solution)/shard_map/reduce_scatter | solution.py:80
  68.7 1.8 copy-start.4
  70.4 156.9 %reduce-scatter.17.cloned.1.call-start = ((), (), s32[]{:S(2)}) async-start(), calls=%async_computation.6 | async-start | bytes 1769472 | tf_op jit(solution)/shard_map/reduce_scatter | solution.py:93
  123.3 1.7 copy-start.5
  124.9 277.3 %reduce-scatter.19.cloned.1.call-start = ((), (), s32[]{:S(2)}) async-start(), calls=%async_computation.7 | async-start | bytes 1622016
  279.4 242.8 %reduce-scatter.15.cloned.1.call-start = ((), (), s32[]{:S(2)}) async-start(), calls=%async_computation.5 | async-start | bytes 1622016
  330.4 6.1 %copy-start.2 = (bf16[48,256,128]{2,1,0:T(8,128)(2,1)S(1)}, bf16[48,256,128]{2,1,0:T(8,128)(2,1)}, u32[]{:S(2)}) copy-start(bf16[48,256,128]{2,1,0:T(8,128)(2,1)} %gather_fusion) | copy-start | bytes 9437188
  330.4 6.1 %copy-start.3 = (bf16[48,256,128]{2,1,0:T(8,128)(2,1)S(1)}, bf16[48,256,128]{2,1,0:T(8,128)(2,1)}, u32[]{:S(2)}) copy-start(bf16[48,256,128]{2,1,0:T(8,128)(2,1)} %gather_fusion.3) | copy-start | bytes 9437188
  336.5 187.5 %copy-start.1 = (bf16[1,1,48,128,128]{4,3,2,1,0:T(8,128)(2,1)S(1)}, bf16[1,1,48,128,128]{4,3,2,1,0:T(8,128)(2,1)}, u32[]{:S(2)}) copy-start(bf16[1,1,48,128,128]{4,3,2,1,0:T(8,128)(2,1)} %param.12) | copy-start | bytes 4718596
Sparse Core Ops, SparseCore 0:
  70.5 74.4 reduce-scatter.12
  149.5 77.6 reduce-scatter.16
  279.5 122.6 reduce-scatter.18
  404.6 117.5 reduce-scatter.14
where the time goes:
time: 541 us; the launch traced here: 531 us
  waiting for transfers between devices  283 us (52%)
  blocking collectives  137 us (25%)
  matrix products  50 us (9%)
  local copies, waits for them, and re-layouts  33.4 us (6%)
  between operations  14.6 us (3%)
  other arithmetic  12.4 us (2%)
    unnamed x6, waiting for transfers between devices  181 us
    reduce_scatter x1, waiting for transfers between devices, local(): lax.psum_scatter(sparse_apply(rows_part, second_blocks, w2_cols, w2_rows,...  82.3 us
    all_gather x1, blocking collectives, local(): lax.all_gather(tokens, 'col', axis=0, tiled=True)  40.9 us
    all_gather x1, blocking collectives, local(): lax.all_gather(cotangent, 'col', axis=0, tiled=True)  33.2 us
    all_gather x1, blocking collectives, local(): lax.all_gather((grad_act * gelu_slope(hidden)).astype(jnp.bfloat16), 'row...  32 us
    all_gather x1, blocking collectives, local(): lax.all_gather(gelu_value(hidden).astype(jnp.bfloat16), 'row', axis=0, ti...  31.3 us
    dot_general x4, matrix products, sparse_apply(): jnp.einsum('ktc,ko->toc', products, placement_table, precision=lax.Precis...  28.2 us
    reduce_scatter x1, waiting for transfers between devices, local(): lax.psum_scatter(sparse_apply(rows_part, first_blocks, w1_rows, w1_cols,...  20 us
  transfers between devices with their start and end apart: 4, of which 4 were waited for; matrix products, arithmetic and copies ran while one was open for 10% of the time, Pallas kernels for 0%

commit v1 on v0

v1 whole, which is shorter than its diff:
```python
import functools
import math

import jax
import jax.numpy as jnp
from jax import lax
from jax.experimental import pallas as pl
from jax.experimental.pallas import tpu as pltpu
from jax.sharding import PartitionSpec as P

MESH = pl.DeviceIdType.MESH
BLK = 128
NCH = 3
F32 = jnp.float32
BF16 = jnp.bfloat16
SLOPE = math.sqrt(2.0 / math.pi)
Z_ORDER = (4, 3, 5, 2, 6, 1, 7)
Z_WAIT = (1, 7, 2, 6, 3, 5, 4)
ROW_ORDER = ((2, 1), (1, 1), (3, 1), (0, 1), (2, 0), (1, 0), (3, 0))


def dot_nn(a, b):
    return jnp.dot(a, b, preferred_element_type=F32)


def dot_nt(a, b):
    return lax.dot_general(a, b, (((1,), (1,)), ((), ())), preferred_element_type=F32)


def mega(
    tok, cot, m1, m2, bias, w1, w2,
    out_o, tg_o, t_o, c_o, a_o, g_o,
    t_all, c_all, a_all, g_all, w1d, w2d, wb1, wb2,
    h_send, ga_send, h_recv, ga_recv, slope_s,
    s_send, s_recv, own_a, b_send, b_recv, own_b, z_send, z_recv,
    loc, zs, zr, xs, xr, bs, br, rs_s, rs_r, ag_s, ag_r, la_s, la_r, lb_s, lb_r, lc_s, lc_r,
):
    rows = tok.shape[0]
    width = tok.shape[1]
    cw = width // NCH
    row, col = lax.axis_index("row"), lax.axis_index("col")
    y, xh = row // 2, row % 2
    z, xl, k = col // 4, (col // 2) % 2, col % 2

    def col_dev(zz, xx, kk):
        return (row, zz * 4 + xx * 2 + kk)

    def row_dev(dy, dx):
        return (((y + dy) % 4) * 2 + (xh + dx) % 2, col)

    def at_pos(zz, xx, kk):
        return kk * 16 + xx * 8 + zz

    def send(src, dst, ssem, rsem, dev):
        return pltpu.make_async_remote_copy(
            src_ref=src, dst_ref=dst, send_sem=ssem, recv_sem=rsem, device_id=dev, device_id_type=MESH
        )

    sib = col_dev(z, xl, 1 - k)
    xnb = col_dev(z, 1 - xl, k)
    peers = [row_dev(dy, dx) for dy, dx in ROW_ORDER]
    peers += [col_dev((z + d) % 8, xl, k) for d in range(1, 8)] + [sib, xnb]

    load1 = pltpu.make_async_copy(w1, wb1, loc.at[0])
    load2 = pltpu.make_async_copy(w2, wb2, loc.at[1])
    load1.start()
    load2.start()
    bar = pltpu.get_barrier_semaphore()
    for dev in peers:
        pl.semaphore_signal(bar, inc=1, device_id=dev, device_id_type=MESH)

    def densify(mask, blocks, dense):
        cap = blocks.shape[0]
        tr, tc = mask.shape

        def one_row(i, slot):
            for j in range(tc):
                live = mask[i, j]
                block = blocks[jnp.minimum(slot, cap - 1)]
                dense[pl.ds(pl.multiple_of(i * BLK, BLK), BLK), j * BLK:(j + 1) * BLK] = jnp.where(
                    live > 0, block, jnp.zeros_like(block)
                )
                slot = slot + live
            return slot

        lax.fori_loop(0, tr, one_row, jnp.int32(0))

    load1.wait()
    densify(m1, wb1, w1d)
    pl.semaphore_wait(bar, len(peers))

    pend = []

    ins, fulls = (tok, cot), (t_all, c_all)
    mine = at_pos(z, xl, k)
    zc, xc, bc, own = {}, {}, {}, {}
    for a in range(2):
        src, full = ins[a], fulls[a]
        for d in Z_ORDER:
            zc[a, d] = send(src, full.at[mine], zs.at[a, d], zr.at[a, d], col_dev((z + d) % 8, xl, k))
            zc[a, d].start()
        xc[a, 0] = send(src, full.at[mine], xs.at[a, 0], xr.at[a, 0], xnb)
        xc[a, 0].start()
        bc[a, 0] = send(src, full.at[mine], bs.at[a, 0], br.at[a, 0], sib)
        bc[a, 0].start()
        own[a] = pltpu.make_async_copy(src, full.at[mine], loc.at[2 + a])
        own[a].start()
    load2.wait()
    densify(m2, wb2, w2d)

    def forward_z(a):
        full = fulls[a]
        for d in Z_WAIT:
            zc[a, d].wait_recv()
            got = full.at[at_pos((z - d + 8) % 8, xl, k)]
            xc[a, d] = send(got, got, xs.at[a, d], xr.at[a, d], xnb)
            xc[a, d].start()
            bc[a, d] = send(got, got, bs.at[a, d], br.at[a, d], sib)
            bc[a, d].start()

    def forward_x(a):
        full = fulls[a]
        for d in (0,) + Z_WAIT:
            xc[a, d].wait_recv()
            got = full.at[at_pos((z - d + 8) % 8, 1 - xl, k)]
            bc[a, 8 + d] = send(got, got, bs.at[a, 8 + d], br.at[a, 8 + d], sib)
            bc[a, 8 + d].start()

    def finish(a):
        own[a].wait()
        for d in range(16):
            bc[a, d].wait_recv()

    def cols(n):
        return pl.ds(pl.multiple_of(n * cw, cw), cw)

    def share(dy, dx):
        return pl.ds(pl.multiple_of(row_dev(dy, dx)[0] * 32, 32), 32)

    my_share = pl.ds(pl.multiple_of(row * 32, 32), 32)

    def scatter_copy(w, n, i):
        buf, got = ((h_send, h_recv), (ga_send, ga_recv))[w]
        dy, dx = ROW_ORDER[i]
        return send(
            buf.at[n, share(dy, dx)], got.at[i, n],
            rs_s.at[w, n, i], rs_r.at[w, n, i], row_dev(dy, dx),
        )

    def gather_copy(w, n, i):
        full = (a_all, g_all)[w]
        dy, dx = ROW_ORDER[i]
        ref = full.at[n, my_share]
        return send(ref, ref, ag_s.at[w, n, i], ag_r.at[w, n, i], row_dev(dy, dx))

    def loop(body):
        lax.fori_loop(0, NCH, lambda n, c: (body(n), c)[1], 0)

    def hidden_part(n):
        h_send[n] = dot_nn(t_all[...].reshape(256, width), w1d[:, cols(n)]).astype(BF16)
        for i in range(7):
            scatter_copy(0, n, i).start()

    def grad_part(n):
        ga_send[n] = dot_nt(c_all[...].reshape(256, width), w2d[cols(n), :]).astype(BF16)
        for i in range(7):
            scatter_copy(1, n, i).start()

    def summed(w, n):
        buf, got = ((h_send, h_recv), (ga_send, ga_recv))[w]
        total = buf[n, my_share, :].astype(F32)
        for i in range(7):
            scatter_copy(w, n, i).wait_recv()
        for i in range(7):
            total = total + got[i, n].astype(F32)
        return total

    def act_part(n):
        v = summed(0, n) + bias[:, cols(n)]
        t = jnp.tanh(SLOPE * (v + 0.044715 * v * v * v))
        a_all[n, my_share, :] = (0.5 * v * (1.0 + t)).astype(BF16)
        slope_s[n] = 0.5 * (1.0 + t) + 0.5 * v * (1.0 - t * t) * SLOPE * (
            1.0 + 3.0 * 0.044715 * v * v
        )
        for i in range(7):
            gather_copy(0, n, i).start()

    def gh_part(n):
        g_all[n, my_share, :] = (summed(1, n) * slope_s[n]).astype(BF16)
        for i in range(7):
            gather_copy(1, n, i).start()

    def gathered(w):
        def body(n):
            for i in range(7):
                gather_copy(w, n, i).wait_recv()

        loop(body)

    forward_z(0)
    forward_x(0)
    finish(0)
    loop(hidden_part)
    forward_z(1)
    forward_x(1)
    finish(1)
    loop(grad_part)
    loop(act_part)
    loop(gh_part)

    def quarter(kk, xx):
        return pl.ds(pl.multiple_of(kk * 128 + xx * 64, 64), 64)

    def eighth(zz):
        return pl.ds(pl.multiple_of(zz * 8, 8), 8)

    def copy_a(w, n):
        return send(s_send.at[w, n], s_recv.at[w, n], la_s.at[w, n], la_r.at[w, n], sib)

    def copy_b(w, n):
        return send(b_send.at[w, n], b_recv.at[w, n], lb_s.at[w, n], lb_r.at[w, n], xnb)

    def copy_c(w, n, d):
        zz = (z + d) % 8
        return send(
            z_send.at[w, n, zz], z_recv.at[w, n, d], lc_s.at[w, n, d], lc_r.at[w, n, d], col_dev(zz, xl, k)
        )

    def level_a(w):
        full = (a_all, g_all)[w]

        def body(n):
            part = None
            for c in range(NCH):
                left = jnp.concatenate(
                    [full[c, quarter(kk, xx), :] for kk in (1 - k, k) for xx in (1 - xl, xl)], axis=0
                )
                deep = slice(c * cw, (c + 1) * cw)
                term = dot_nn(left, w2d[deep, cols(n)]) if w == 0 else dot_nt(left, w1d[cols(n), deep])
                part = term if part is None else part + term
            s_send[w, n] = part[:128].reshape(2, 64, cw).astype(BF16)
            own_a[w, n] = part[128:].reshape(2, 64, cw)
            copy_a(w, n).start()

        loop(body)

    def level_b(w):
        def body(n):
            copy_a(w, n).wait_recv()
            b_send[w, n] = (own_a[w, n, 0] + s_recv[w, n, 0].astype(F32)).astype(BF16)
            copy_b(w, n).start()
            own_b[w, n] = own_a[w, n, 1] + s_recv[w, n, 1].astype(F32)

        loop(body)

    def level_c(w):
        def body(n):
            copy_b(w, n).wait_recv()
            total = own_b[w, n] + b_recv[w, n].astype(F32)
            own_b[w, n] = total
            z_send[w, n] = total.reshape(8, rows, cw).astype(BF16)
            for d in Z_ORDER:
                copy_c(w, n, d).start()

        loop(body)

    def last(w):
        for n in range(NCH):
            total = own_b[w, n, eighth(z), :]
            for d in Z_WAIT:
                copy_c(w, n, d).wait_recv()
            for d in range(1, 8):
                total = total + z_recv[w, n, d].astype(F32)
            (out_o, tg_o)[w][:, n * cw:(n + 1) * cw] = total.astype(BF16)

    stores = [pltpu.make_async_copy(t_all, t_o, loc.at[4]), pltpu.make_async_copy(c_all, c_o, loc.at[5])]
    for s in stores:
        s.start()
    gathered(0)
    stores.append(pltpu.make_async_copy(a_all, a_o, loc.at[6]))
    stores[-1].start()
    level_a(0)
    level_b(0)
    gathered(1)
    stores.append(pltpu.make_async_copy(g_all, g_o, loc.at[7]))
    stores[-1].start()
    level_a(1)
    level_c(0)
    level_b(1)
    last(0)
    level_c(1)
    last(1)

    for table in (zc, xc, bc):
        for copy in table.values():
            copy.wait_send()
    for w in range(2):
        def drain(n):
            for i in range(7):
                scatter_copy(w, n, i).wait_send()
                gather_copy(w, n, i).wait_send()
            copy_a(w, n).wait_send()
            copy_b(w, n).wait_send()
            for d in range(1, 8):
                copy_c(w, n, d).wait_send()

        loop(drain)
    for s in stores:
        s.wait()


def block_grads(
    m1, m2, t, c, a, g, out_i, tg_i, g1_o, g2_o, out_o, tg_o, bg_o, i1, i2, count
):
    step = pl.program_id(0)
    per = g1_o.shape[0]

    @pl.when(step == 0)
    def _():
        out_o[...] = out_i[...]
        tg_o[...] = tg_i[...]
        bg_o[...] = jnp.concatenate(
            [jnp.sum(g[n].astype(F32), axis=0, keepdims=True) for n in range(NCH)], axis=1
        )
        for which, (mask, table) in enumerate(((m1, i1), (m2, i2))):
            tr, tc = mask.shape

            def one_row(i, slot):
                for j in range(tc):
                    table[slot] = i * tc + j
                    slot = slot + mask[i, j]
                return slot

            count[which] = lax.fori_loop(0, tr, one_row, jnp.int32(0))

    def flat(ref, i):
        return ref[:, pl.ds(pl.multiple_of(i * BLK, BLK), BLK)]

    def chunked(ref, i):
        each = ref.shape[2] // BLK
        return ref[i // each, :, pl.ds(pl.multiple_of(i % each * BLK, BLK), BLK)]

    def one_slot(s, carry):
        slot = step * per + s
        for which, (mask, table, dest) in enumerate(((m1, i1, g1_o), (m2, i2, g2_o))):
            tc = mask.shape[1]
            live = slot < count[which]
            place = jnp.where(live, table[slot], 0)
            r, q = place // tc, place % tc
            lb, rb = (flat(t, r), chunked(g, q)) if which == 0 else (chunked(a, r), flat(c, q))
            grad = lax.dot_general(lb, rb, (((0,), (0,)), ((), ())), preferred_element_type=F32)
            dest[s] = jnp.where(live, grad, 0.0)
        return carry

    lax.fori_loop(0, per, one_slot, 0, unroll=True)


def local(tokens, cotangent, w1_mask, w1_blocks, bias, w2_mask, w2_blocks):
    rows, width = tokens.shape
    total = 256
    cap = w1_blocks.shape[2]
    w1b = w1_blocks.reshape(w1_blocks.shape[2:])
    w2b = w2_blocks.reshape(w2_blocks.shape[2:])
    wide = bias.astype(F32).reshape(1, -1)
    vmem = pl.BlockSpec(memory_space=pltpu.VMEM)
    smem = pl.BlockSpec(memory_space=pltpu.SMEM)
    anyw = pl.BlockSpec(memory_space=pl.ANY)
    full = jax.ShapeDtypeStruct((NCH, total, width // NCH), BF16)
    small = jax.ShapeDtypeStruct((rows, width), BF16)
    dma = pltpu.SemaphoreType.DMA
    V = pltpu.VMEM
    cw = width // NCH
    tall = jax.ShapeDtypeStruct((total // rows, rows, width), BF16)
    out, tg, t, c, a, g = pl.pallas_call(
        mega,
        name="mega",
        out_shape=(small, small, tall, tall, full, full),
        in_specs=[vmem, vmem, smem, smem, vmem, anyw, anyw],
        out_specs=(vmem, vmem, anyw, anyw, anyw, anyw),
        scratch_shapes=[
            V((total // rows, rows, width), BF16), V((total // rows, rows, width), BF16),
            V((NCH, total, cw), BF16), V((NCH, total, cw), BF16),
            V((width, width), BF16), V((width, width), BF16),
            V((cap, BLK, BLK), BF16), V((cap, BLK, BLK), BF16),
            V((NCH, total, cw), BF16), V((NCH, total, cw), BF16),
            V((7, NCH, 32, cw), BF16), V((7, NCH, 32, cw), BF16), V((NCH, 32, cw), F32),
            V((2, NCH, 2, 64, cw), BF16), V((2, NCH, 2, 64, cw), BF16), V((2, NCH, 2, 64, cw), F32),
            V((2, NCH, 64, cw), BF16), V((2, NCH, 64, cw), BF16), V((2, NCH, 64, cw), F32),
            V((2, NCH, 8, rows, cw), BF16), V((2, NCH, 8, rows, cw), BF16),
            dma((8,)), dma((2, 8)), dma((2, 8)), dma((2, 8)), dma((2, 8)), dma((2, 16)), dma((2, 16)),
            dma((2, NCH, 7)), dma((2, NCH, 7)), dma((2, NCH, 7)), dma((2, NCH, 7)),
            dma((2, NCH)), dma((2, NCH)), dma((2, NCH)), dma((2, NCH)), dma((2, NCH, 8)), dma((2, NCH, 8)),
        ],
        compiler_params=pltpu.CompilerParams(
            collective_id=0, has_side_effects=True, vmem_limit_bytes=48 * 1024 * 1024
        ),
    )(tokens, cotangent, w1_mask, w2_mask, wide, w1b, w2b)

    per = 8
    whole = lambda shape: pl.BlockSpec(shape, lambda i: tuple(0 for _ in shape))
    mask_spec = smem
    slot_spec = pl.BlockSpec((per, BLK, BLK), lambda i: (i, 0, 0))
    grads = jax.ShapeDtypeStruct((cap, BLK, BLK), F32)
    g1, g2, out, tg, bg = pl.pallas_call(
        block_grads,
        name="block_grads",
        grid=(cap // per,),
        out_shape=(grads, grads, small, small, jax.ShapeDtypeStruct((1, width), F32)),
        in_specs=[mask_spec, mask_spec] + [whole((total, width))] * 2 + [whole((NCH, total, cw))] * 2 + [whole((rows, width))] * 2,
        out_specs=(slot_spec, slot_spec, whole((rows, width)), whole((rows, width)), whole((1, width))),
        scratch_shapes=[
            pltpu.SMEM((cap + 8,), jnp.int32), pltpu.SMEM((cap + 8,), jnp.int32), pltpu.SMEM((2,), jnp.int32)
        ],
    )(w1_mask, w2_mask, t.reshape(total, width), c.reshape(total, width), a, g, out, tg)
    return out, tg, g1[None, None], g2[None, None], bg.reshape(-1)


def solution(mesh):
    weights = P("row", "col", None, None, None)
    return jax.shard_map(
        local,
        mesh=mesh,
        in_specs=(P("col", "row"), P("col", "row"), P("row", "col"), weights, P("col"), P("col", "row"), weights),
        out_specs=(P("col", "row"), P("col", "row"), weights, weights, P("col")),
        check_vma=False,
    )
```

time: 541 us -> 106 us (0.20); the launches traced: 531 us -> 104 us
  waiting for transfers between devices: 283 us -> 0 us
  blocking collectives: 137 us -> 0 us
  Pallas kernels: 0 us -> 92.7 us
  matrix products: 50 us -> 0 us
  local copies, waits for them, and re-layouts: 33.4 us -> 9.73 us
  between operations: 14.6 us -> 0.66 us
  other arithmetic: 12.4 us -> 1.31 us
    unnamed x6 -> x0, waiting for transfers between devices: 181 us -> none
    all_gather x4 -> x0, blocking collectives: 137 us -> none  [the longest x1 40.9 us: local(): lax.all_gather(tokens, 'col', axis=0, tiled=True)]
    reduce_scatter x2 -> x0, waiting for transfers between devices: 102 us -> none  [the longest x1 82.3 us: local(): lax.psum_scatter(sparse_apply(rows_part, second_blocks, w2_cols, w2_rows,...]
    pallas_call x0 -> x2, Pallas kernels: none -> 92.7 us  [the longest x1 84.7 us: local(): pl.pallas_call(mega, name='mega', out_shape=(small, small, tall, tall, fu...]
    dot_general x10 -> x0, matrix products: 50 us -> none  [the longest x4 28.2 us: sparse_apply(): jnp.einsum('ktc,ko->toc', products, placement_table, precision=lax.Precis...]
    gather x4 -> x0, local copies, waits for them, and re-layouts: 10.9 us -> none  [sparse_apply(): picked = jnp.take(pieces, source, axis=1)]
    transpose x4 -> x0, local copies, waits for them, and re-layouts: 7.67 us -> none  [sparse_apply(): jnp.einsum('ktc,ko->toc', products, placement_table, precision=lax.Precis...]
    sort x2 -> x0, other arithmetic: 6.34 us -> none  [slot_layout(): order = jnp.argsort(1 - flat, stable=True)[:capacity]]
  transfers between devices with their start and end apart: 4 -> 0, of which waited for: 4 -> 0; matrix products, arithmetic and copies ran while one was open for 10% -> 0% of each run, Pallas kernels for 0% -> 0%
where the time goes in v1:
time: 106 us; the launch traced here: 104 us
  Pallas kernels  92.7 us (87%)
  local copies, waits for them, and re-layouts  9.73 us (9%)
  other arithmetic  1.31 us (1%)
    pallas_call x1, Pallas kernels, local(): pl.pallas_call(mega, name='mega', out_shape=(small, small, tall, tall, fu...  84.7 us
    unnamed x22, local copies, waits for them, and re-layouts  9.04 us
    pallas_call x1, Pallas kernels, local(): pl.pallas_call(block_grads, name='block_grads', grid=(cap // per,), out_s...  7.97 us

profile of v1, /device:TPU:1, one launch (start us, length us, event | category | flops | bytes accessed | tf_op | source)
XLA Modules:
  0.0 104.4 jit_solution(1092678680376465976)
XLA Ops:
  0.6 0.7 reshape.38.bias
  1.3 0.0 copy-start
  1.3 1.4 %copy-done = bf16[1,1,48,128,128]{4,3,2,1,0:T(8,128)(2,1)S(1)} copy-done((bf16[1,1,48,128,128]{4,3,2,1,0:T(8,128)(2,1)S(1)}, bf16[1,1,48,128,128]{4,3,2,1,0:T(8,128)(2,1)}, u32[]{:S(2)}) %copy-start) | copy-done | bytes 1572888
  2.7 0.0 copy-start.5
  2.7 0.7 copy-done.5
  3.4 0.0 copy-start.6
  3.4 0.7 copy-done.6
  4.1 0.0 copy-start.7
  4.1 0.7 copy-done.7
  4.9 0.0 copy-start.8
  4.9 0.7 copy-done.8
  5.6 84.7 %mega.1 = (bf16[8,1536]{1,0:T(8,128)(2,1)S(1)}, bf16[8,1536]{1,0:T(8,128)(2,1)S(1)}, bf16[32,8,1536]{2,1,0:T(8,128)(2,1)S(1)}, bf16[32,8,1536]{2,1,0:T(8,128)(2,...) custom-call(bf16[8,1536]{1,0:T(8,128)(2,1)S(1)} %copy-done.7, bf16[8,1536]{1,0:T(8,128)(2,1)S(1)} %copy-done.8, ...), custom_call_target="tpu_custom_call" | custom-call | tf_op jit(solution)/shard_map/mega/pallas_call | solution.py:374
  90.4 0.0 copy-start.1
  90.4 0.9 copy-done.1
  91.2 0.0 copy-start.2
  91.2 0.9 copy-done.2
  92.2 0.0 copy-start.3
  92.2 0.9 copy-done.3
  93.0 0.0 copy-start.4
  93.0 0.9 copy-done.4
  93.9 0.0 copy-start.9
  93.9 0.6 copy-done.9
  94.5 0.0 copy-start.10
  94.5 0.6 copy-done.10
  95.1 8.0 %block_grads.1 = (f32[48,128,128]{2,1,0:T(8,128)}, f32[48,128,128]{2,1,0:T(8,128)}, bf16[8,1536]{1,0:T(8,128)(2,1)}, bf16[8,1536]{1,0:T(8,128)(2,1)}, f32[1,1536]{1,0:T(1,128)}) custom-call(s32[12,12]{1,0:T(8,128)} %m1.3, s32[12,12]{1,0:T(8,128)} %m2.3, bf16[256,1536]{1,0:T(8,128)(2,1)} %bitcast.7, bf16[256,1536]{1,0:T(8,128)(2,1)} %bitcast.8, ...), custom_call_target="tpu_custom_call" | custom-call | tf_op jit(solution)/shard_map/block_grads/pallas_call | solution.py:404
  103.1 1.3 %reduce = f32[1536]{0:T(1024)} reduce(f32[1,1536]{1,0:T(1,128)} %get-tuple-element.26, f32[]{:T(128)} %constant.6), dimensions={0}, to_apply=%get-tuple-element.26.reduce_sub_computation | reduce | bytes 12292 | tf_op jit(solution)/shard_map/block_grads/pallas_call | solution.py:404
Async XLA Ops:
  1.3 1.4 %copy-start = (bf16[1,1,48,128,128]{4,3,2,1,0:T(8,128)(2,1)S(1)}, bf16[1,1,48,128,128]{4,3,2,1,0:T(8,128)(2,1)}, u32[]{:S(2)}) copy-start(bf16[1,1,48,128,128]{4,3,2,1,0:T(8,128)(2,1)} %param.10) | copy-start | bytes 4718596
  2.7 0.7 copy-start.5
  3.4 0.7 copy-start.6
  4.1 0.7 copy-start.7
  4.9 0.7 copy-start.8
  90.4 0.9 copy-start.1
  91.2 0.9 copy-start.2
  92.2 0.9 copy-start.3
  93.0 0.9 copy-start.4
  93.9 0.6 copy-start.9
  94.5 0.6 copy-start.10

commit v2 on v1

--- a/solution.py
+++ b/solution.py
@@ -32,7 +32,7 @@
     out_o, tg_o, t_o, c_o, a_o, g_o,
     t_all, c_all, a_all, g_all, w1d, w2d, wb1, wb2,
     h_send, ga_send, h_recv, ga_recv, slope_s,
-    s_send, s_recv, own_a, b_send, b_recv, own_b, z_send, z_recv,
+    bias_s, s_send, s_recv, own_a, b_send, b_recv, own_b, z_send, z_recv, t_turn, a_turn,
     loc, zs, zr, xs, xr, bs, br, rs_s, rs_r, ag_s, ag_r, la_s, la_r, lb_s, lb_r, lc_s, lc_r,
 ):
     rows = tok.shape[0]
@@ -105,6 +105,7 @@
         bc[a, 0].start()
         own[a] = pltpu.make_async_copy(src, full.at[mine], loc.at[2 + a])
         own[a].start()
+    bias_s[...] = bias[...].astype(F32).reshape(1, width)
     load2.wait()
     densify(m2, wb2, w2d)
 
@@ -176,7 +177,7 @@
         return total
 
     def act_part(n):
-        v = summed(0, n) + bias[:, cols(n)]
+        v = summed(0, n) + bias_s[:, cols(n)]
         t = jnp.tanh(SLOPE * (v + 0.044715 * v * v * v))
         a_all[n, my_share, :] = (0.5 * v * (1.0 + t)).astype(BF16)
         slope_s[n] = 0.5 * (1.0 + t) + 0.5 * v * (1.0 - t * t) * SLOPE * (
@@ -197,14 +198,31 @@
 
         loop(body)
 
+    stores = []
+
+    def store(src, dst):
+        stores.append(pltpu.make_async_copy(src, dst, loc.at[4 + len(stores)]))
+        stores[-1].start()
+
+    def turn(n):
+        t_turn[pl.ds(pl.multiple_of(n * cw, cw), cw), :] = (
+            t_all[:, :, cols(n)].reshape(256, cw).astype(F32).T.astype(BF16)
+        )
+
+    def turn_act(n):
+        a_turn[pl.ds(pl.multiple_of(n * cw, cw), cw), :] = a_all[n].astype(F32).T.astype(BF16)
+
     forward_z(0)
     forward_x(0)
+    forward_z(1)
     finish(0)
     loop(hidden_part)
-    forward_z(1)
     forward_x(1)
     finish(1)
     loop(grad_part)
+    loop(turn)
+    store(t_turn, t_o)
+    store(c_all, c_o)
     loop(act_part)
     loop(gh_part)
 
@@ -273,22 +291,18 @@
                 total = total + z_recv[w, n, d].astype(F32)
             (out_o, tg_o)[w][:, n * cw:(n + 1) * cw] = total.astype(BF16)
 
-    stores = [pltpu.make_async_copy(t_all, t_o, loc.at[4]), pltpu.make_async_copy(c_all, c_o, loc.at[5])]
-    for s in stores:
-        s.start()
     gathered(0)
-    stores.append(pltpu.make_async_copy(a_all, a_o, loc.at[6]))
-    stores[-1].start()
     level_a(0)
     level_b(0)
+    loop(turn_act)
+    store(a_turn, a_o)
     gathered(1)
-    stores.append(pltpu.make_async_copy(g_all, g_o, loc.at[7]))
-    stores[-1].start()
     level_a(1)
+    store(g_all, g_o)
     level_c(0)
     level_b(1)
+    level_c(1)
     last(0)
-    level_c(1)
     last(1)
 
     for table in (zc, xc, bc):
@@ -310,18 +324,21 @@
 
 
 def block_grads(
-    m1, m2, t, c, a, g, out_i, tg_i, g1_o, g2_o, out_o, tg_o, bg_o, i1, i2, count
+    m1, m2, t_h, c_h, a_h, g_h, out_i, tg_i, g1_o, g2_o, out_o, tg_o, bg_o, t, c, a, g, i1, i2, count, sems
 ):
     step = pl.program_id(0)
     per = g1_o.shape[0]
 
     @pl.when(step == 0)
     def _():
+        loads = [
+            pltpu.make_async_copy(src, dst, sems.at[i])
+            for i, (src, dst) in enumerate(((g_h, g), (t_h, t), (a_h, a), (c_h, c)))
+        ]
+        for load in loads:
+            load.start()
         out_o[...] = out_i[...]
         tg_o[...] = tg_i[...]
-        bg_o[...] = jnp.concatenate(
-            [jnp.sum(g[n].astype(F32), axis=0, keepdims=True) for n in range(NCH)], axis=1
-        )
         for which, (mask, table) in enumerate(((m1, i1), (m2, i2))):
             tr, tc = mask.shape
 
@@ -332,27 +349,31 @@
                 return slot
 
             count[which] = lax.fori_loop(0, tr, one_row, jnp.int32(0))
-
-    def flat(ref, i):
-        return ref[:, pl.ds(pl.multiple_of(i * BLK, BLK), BLK)]
-
-    def chunked(ref, i):
-        each = ref.shape[2] // BLK
-        return ref[i // each, :, pl.ds(pl.multiple_of(i % each * BLK, BLK), BLK)]
-
-    def one_slot(s, carry):
+        for load in loads:
+            load.wait()
+        cw = g.shape[2]
+        for n in range(NCH):
+            bg_o[n * cw:(n + 1) * cw] = jnp.sum(g[n].astype(F32), axis=0)
+
+    def tall(ref, i):
+        return ref[pl.ds(pl.multiple_of(i * BLK, BLK), BLK), :]
+
+    def cot(i):
+        return c[:, :, pl.ds(pl.multiple_of(i * BLK, BLK), BLK)].reshape(256, BLK)
+
+    def hid(i):
+        each = g.shape[2] // BLK
+        return g[i // each, :, pl.ds(pl.multiple_of(i % each * BLK, BLK), BLK)]
+
+    for s in range(per):
         slot = step * per + s
         for which, (mask, table, dest) in enumerate(((m1, i1, g1_o), (m2, i2, g2_o))):
             tc = mask.shape[1]
             live = slot < count[which]
             place = jnp.where(live, table[slot], 0)
             r, q = place // tc, place % tc
-            lb, rb = (flat(t, r), chunked(g, q)) if which == 0 else (chunked(a, r), flat(c, q))
-            grad = lax.dot_general(lb, rb, (((0,), (0,)), ((), ())), preferred_element_type=F32)
+            grad = dot_nn(tall(t, r), hid(q)) if which == 0 else dot_nn(tall(a, r), cot(q))
             dest[s] = jnp.where(live, grad, 0.0)
-        return carry
-
-    lax.fori_loop(0, per, one_slot, 0, unroll=True)
 
 
 def local(tokens, cotangent, w1_mask, w1_blocks, bias, w2_mask, w2_blocks):
@@ -361,7 +382,6 @@
     cap = w1_blocks.shape[2]
     w1b = w1_blocks.reshape(w1_blocks.shape[2:])
     w2b = w2_blocks.reshape(w2_blocks.shape[2:])
-    wide = bias.astype(F32).reshape(1, -1)
     vmem = pl.BlockSpec(memory_space=pltpu.VMEM)
     smem = pl.BlockSpec(memory_space=pltpu.SMEM)
     anyw = pl.BlockSpec(memory_space=pl.ANY)
@@ -370,11 +390,12 @@
     dma = pltpu.SemaphoreType.DMA
     V = pltpu.VMEM
     cw = width // NCH
+    turned = jax.ShapeDtypeStruct((width, total), BF16)
     tall = jax.ShapeDtypeStruct((total // rows, rows, width), BF16)
     out, tg, t, c, a, g = pl.pallas_call(
         mega,
         name="mega",
-        out_shape=(small, small, tall, tall, full, full),
+        out_shape=(small, small, turned, tall, turned, full),
         in_specs=[vmem, vmem, smem, smem, vmem, anyw, anyw],
         out_specs=(vmem, vmem, anyw, anyw, anyw, anyw),
         scratch_shapes=[
@@ -383,18 +404,18 @@
             V((width, width), BF16), V((width, width), BF16),
             V((cap, BLK, BLK), BF16), V((cap, BLK, BLK), BF16),
             V((NCH, total, cw), BF16), V((NCH, total, cw), BF16),
-            V((7, NCH, 32, cw), BF16), V((7, NCH, 32, cw), BF16), V((NCH, 32, cw), F32),
+            V((7, NCH, 32, cw), BF16), V((7, NCH, 32, cw), BF16), V((NCH, 32, cw), F32), V((1, width), F32),
             V((2, NCH, 2, 64, cw), BF16), V((2, NCH, 2, 64, cw), BF16), V((2, NCH, 2, 64, cw), F32),
             V((2, NCH, 64, cw), BF16), V((2, NCH, 64, cw), BF16), V((2, NCH, 64, cw), F32),
-            V((2, NCH, 8, rows, cw), BF16), V((2, NCH, 8, rows, cw), BF16),
+            V((2, NCH, 8, rows, cw), BF16), V((2, NCH, 8, rows, cw), BF16), V((width, total), BF16), V((width, total), BF16),
             dma((8,)), dma((2, 8)), dma((2, 8)), dma((2, 8)), dma((2, 8)), dma((2, 16)), dma((2, 16)),
             dma((2, NCH, 7)), dma((2, NCH, 7)), dma((2, NCH, 7)), dma((2, NCH, 7)),
             dma((2, NCH)), dma((2, NCH)), dma((2, NCH)), dma((2, NCH)), dma((2, NCH, 8)), dma((2, NCH, 8)),
         ],
         compiler_params=pltpu.CompilerParams(
-            collective_id=0, has_side_effects=True, vmem_limit_bytes=48 * 1024 * 1024
+            collective_id=0, has_side_effects=True, vmem_limit_bytes=67043328
         ),
-    )(tokens, cotangent, w1_mask, w2_mask, wide, w1b, w2b)
+    )(tokens, cotangent, w1_mask, w2_mask, bias, w1b, w2b)
 
     per = 8
     whole = lambda shape: pl.BlockSpec(shape, lambda i: tuple(0 for _ in shape))
@@ -405,14 +426,18 @@
         block_grads,
         name="block_grads",
         grid=(cap // per,),
-        out_shape=(grads, grads, small, small, jax.ShapeDtypeStruct((1, width), F32)),
-        in_specs=[mask_spec, mask_spec] + [whole((total, width))] * 2 + [whole((NCH, total, cw))] * 2 + [whole((rows, width))] * 2,
-        out_specs=(slot_spec, slot_spec, whole((rows, width)), whole((rows, width)), whole((1, width))),
+        out_shape=(grads, grads, small, small, jax.ShapeDtypeStruct((width,), F32)),
+        in_specs=[mask_spec, mask_spec] + [anyw] * 4 + [whole((rows, width))] * 2,
+        out_specs=(slot_spec, slot_spec, whole((rows, width)), whole((rows, width)), whole((width,))),
         scratch_shapes=[
-            pltpu.SMEM((cap + 8,), jnp.int32), pltpu.SMEM((cap + 8,), jnp.int32), pltpu.SMEM((2,), jnp.int32)
+            V((width, total), BF16), V((total // rows, rows, width), BF16),
+            V((width, total), BF16), V((NCH, total, cw), BF16),
+            pltpu.SMEM((cap + 8,), jnp.int32), pltpu.SMEM((cap + 8,), jnp.int32), pltpu.SMEM((2,), jnp.int32),
+            dma((4,)),
         ],
-    )(w1_mask, w2_mask, t.reshape(total, width), c.reshape(total, width), a, g, out, tg)
-    return out, tg, g1[None, None], g2[None, None], bg.reshape(-1)
+        compiler_params=pltpu.CompilerParams(vmem_limit_bytes=67043328),
+    )(w1_mask, w2_mask, t, c, a, g, out, tg)
+    return out, tg, g1[None, None], g2[None, None], bg
 
 
 def solution(mesh):

time: 106 us -> 90.1 us (0.85)
  local copies, waits for them, and re-layouts: 9.73 us -> 0 us
  Pallas kernels: 92.7 us -> 87.9 us
  other arithmetic: 1.31 us -> 0 us
    unnamed x22 -> x0, local copies, waits for them, and re-layouts: 9.04 us -> none
    pallas_call x1, Pallas kernels: 84.7 us -> 80 us  [local(): pl.pallas_call(mega, name='mega', out_shape=(small, small, turned, tall,...]
    pallas_call x1 -> x0, other arithmetic: 1.31 us -> none  [local(): pl.pallas_call(block_grads, name='block_grads', grid=(cap // per,), out_s...]
where the time goes in v2:
time: 90.1 us; the launch traced here: 88.5 us
  Pallas kernels  87.9 us (98%)
    pallas_call x1, Pallas kernels, local(): pl.pallas_call(mega, name='mega', out_shape=(small, small, turned, tall,...  80 us
    pallas_call x1, Pallas kernels, local(): pl.pallas_call(block_grads, name='block_grads', grid=(cap // per,), out_s...  7.87 us

profile of v2, /device:TPU:1, one launch (start us, length us, event | category | flops | bytes accessed | tf_op | source)
XLA Modules:
  0.0 88.5 jit_solution(54610057325317895)
XLA Ops:
  0.6 80.0 %mega.1 = (bf16[8,1536]{1,0:T(8,128)(2,1)}, bf16[8,1536]{1,0:T(8,128)(2,1)}, bf16[1536,256]{1,0:T(8,128)(2,1)}, bf16[32,8,1536]{2,1,0:T(8,128)(2,1)}, bf16[1536,...) custom-call(bf16[8,1536]{1,0:T(8,128)(2,1)} %tok.1, bf16[8,1536]{1,0:T(8,128)(2,1)} %cot.1, s32[12,12]{1,0:T(8,128)} %m1.3, ...), custom_call_target="tpu_custom_call" | custom-call | tf_op jit(solution)/shard_map/mega/pallas_call | solution.py:395
  80.6 7.9 %block_grads.1 = (f32[48,128,128]{2,1,0:T(8,128)}, f32[48,128,128]{2,1,0:T(8,128)}, bf16[8,1536]{1,0:T(8,128)(2,1)}, bf16[8,1536]{1,0:T(8,128)(2,1)}, f32[1536]{0:T(1024)}) custom-call(s32[12,12]{1,0:T(8,128)} %m1.3, s32[12,12]{1,0:T(8,128)} %m2.3, bf16[1536,256]{1,0:T(8,128)(2,1)} %get-tuple-element.16.t_h, bf16[32,8,1536]{2,1,0:T(8,128)(2,1)} %get-tuple-element.17.c_h, ...), custom_call_target="tpu_custom_call" | custom-call | tf_op jit(solution)/shard_map/block_grads/pallas_call | solution.py:425

commit v3 on v2

v3 whole, which is shorter than its diff:
```python
import functools
import math

import jax
import jax.numpy as jnp
from jax import lax
from jax.experimental import pallas as pl
from jax.experimental.pallas import tpu as pltpu
from jax.sharding import PartitionSpec as P

MESH = pl.DeviceIdType.MESH
BLK = 128
GROUP = 4
NCH = 3
F32 = jnp.float32
BF16 = jnp.bfloat16
SLOPE = math.sqrt(2.0 / math.pi)
Z_ORDER = (4, 3, 5, 2, 6, 1, 7)
Z_WAIT = (1, 7, 2, 6, 3, 5, 4)
ROW_ORDER = ((2, 1), (1, 1), (3, 1), (0, 1), (2, 0), (1, 0), (3, 0))


def dot_nn(a, b):
    return jnp.dot(a, b, preferred_element_type=F32)


def dot_nt(a, b):
    return lax.dot_general(a, b, (((1,), (1,)), ((), ())), preferred_element_type=F32)


def mega(
    tok, cot, m1, m2, bias, w1, w2,
    out_o, tg_o, t_o, c_o, a_o, g_o,
    t_all, c_all, a_all, g_all, w1d, w2d, wb1, wb2,
    h_send, ga_send, h_recv, ga_recv, slope_s, bias_s,
    a_send, a_recv, own_there, own_here, b_send, b_recv, z_send, z_recv, t_turn, a_turn,
    loc, zs, zr, xs, xr, bs, br, rs_s, rs_r, ag_s, ag_r, la_s, la_r, lb_s, lb_r, lc_s, lc_r,
):
    width = tok.shape[1]
    cw = width // NCH
    row, col = lax.axis_index("row"), lax.axis_index("col")
    y, xh = row // 2, row % 2
    z, xl, k = col // 4, (col // 2) % 2, col % 2

    def col_dev(zz, xx, kk):
        return (row, zz * 4 + xx * 2 + kk)

    def row_dev(dy, dx):
        return (((y + dy) % 4) * 2 + (xh + dx) % 2, col)

    def back(d):
        return (z - d + 8) % 8

    def send(src, dst, ssem, rsem, dev):
        return pltpu.make_async_remote_copy(
            src_ref=src, dst_ref=dst, send_sem=ssem, recv_sem=rsem, device_id=dev, device_id_type=MESH
        )

    sib = col_dev(z, xl, 1 - k)
    xnb = col_dev(z, 1 - xl, k)
    peers = [row_dev(dy, dx) for dy, dx in ROW_ORDER]
    peers += [col_dev((z + d) % 8, xl, k) for d in range(1, 8)] + [sib, xnb]

    load1 = pltpu.make_async_copy(w1, wb1, loc.at[0])
    load2 = pltpu.make_async_copy(w2, wb2, loc.at[1])
    load1.start()
    load2.start()
    bar = pltpu.get_barrier_semaphore()
    for dev in peers:
        pl.semaphore_signal(bar, inc=1, device_id=dev, device_id_type=MESH)

    def densify(mask, blocks, dense):
        cap = blocks.shape[0]
        tr, tc = mask.shape

        def one_row(i, slot):
            for j in range(tc):
                live = mask[i, j]
                block = blocks[jnp.minimum(slot, cap - 1)]
                dense[pl.ds(pl.multiple_of(i * BLK, BLK), BLK), j * BLK:(j + 1) * BLK] = jnp.where(
                    live > 0, block, jnp.zeros_like(block)
                )
                slot = slot + live
            return slot

        lax.fori_loop(0, tr, one_row, jnp.int32(0))

    load1.wait()
    densify(m1, wb1, w1d)
    pl.semaphore_wait(bar, len(peers))

    ins, fulls = (tok, cot), (t_all, c_all)
    zc, xc, bc, own = {}, {}, {}, {}
    for a in range(2):
        src, full = ins[a], fulls[a]
        for d in Z_ORDER:
            zc[a, d] = send(src, full.at[0, z], zs.at[a, d], zr.at[a, d], col_dev((z + d) % 8, xl, k))
            zc[a, d].start()
        xc[a, 0] = send(src, full.at[2, z], xs.at[a, 0], xr.at[a, 0], xnb)
        xc[a, 0].start()
        bc[a, 0] = send(src, full.at[1, z], bs.at[a, 0], br.at[a, 0], sib)
        bc[a, 0].start()
        own[a] = pltpu.make_async_copy(src, full.at[0, z], loc.at[2 + a])
        own[a].start()
    bias_s[...] = bias[...].astype(F32).reshape(1, width)
    load2.wait()
    densify(m2, wb2, w2d)

    def forward_z(a):
        full = fulls[a]
        for d in Z_WAIT:
            zc[a, d].wait_recv()
            got = full.at[0, back(d)]
            xc[a, d] = send(got, full.at[2, back(d)], xs.at[a, d], xr.at[a, d], xnb)
            xc[a, d].start()
            bc[a, d] = send(got, full.at[1, back(d)], bs.at[a, d], br.at[a, d], sib)
            bc[a, d].start()
        own[a].wait()

    def forward_x(a):
        full = fulls[a]
        for d in (0,) + Z_WAIT:
            xc[a, d].wait_recv()
            bc[a, 8 + d] = send(
                full.at[2, back(d)], full.at[3, back(d)], bs.at[a, 8 + d], br.at[a, 8 + d], sib
            )
            bc[a, 8 + d].start()

    def arrived(a, first):
        for d in range(first, first + 8):
            bc[a, d].wait_recv()

    def cols(n):
        return pl.ds(pl.multiple_of(n * cw, cw), cw)

    def loop(body):
        lax.fori_loop(0, NCH, lambda n, c: (body(n), c)[1], 0)

    def scatter_copy(w, q, i):
        buf, got = ((h_send, h_recv), (ga_send, ga_recv))[w]
        dev = row_dev(*ROW_ORDER[i])
        return send(buf.at[q, dev[0]], got.at[q, i], rs_s.at[w, q, i], rs_r.at[w, q, i], dev)

    def gather_copy(w, q, i):
        ref = (a_all, g_all)[w].at[q, row]
        return send(ref, ref, ag_s.at[w, q, i], ag_r.at[w, q, i], row_dev(*ROW_ORDER[i]))

    def scatter(w, quarters):
        full, buf = ((t_all, h_send), (c_all, ga_send))[w]

        def body(n):
            left = jnp.concatenate([full[q].reshape(64, width) for q in quarters], axis=0)
            part = dot_nn(left, w1d[:, cols(n)]) if w == 0 else dot_nt(left, w2d[cols(n), :])
            for at, q in enumerate(quarters):
                buf[q, :, :, cols(n)] = part[at * 64:(at + 1) * 64].reshape(8, 8, cw).astype(BF16)

        loop(body)
        for q in quarters:
            for i in range(7):
                scatter_copy(w, q, i).start()

    def summed(w, q):
        buf, got = ((h_send, h_recv), (ga_send, ga_recv))[w]
        total = buf[q, row].astype(F32)
        for i in range(7):
            scatter_copy(w, q, i).wait_recv()
        for i in range(7):
            total = total + got[q, i].astype(F32)
        return total

    def spread(w, q, value):
        (a_all, g_all)[w][q, row] = value.astype(BF16)
        for i in range(7):
            gather_copy(w, q, i).start()

    def act_part(q):
        v = summed(0, q) + bias_s[...]
        t = jnp.tanh(SLOPE * (v + 0.044715 * v * v * v))
        spread(0, q, 0.5 * v * (1.0 + t))
        slope_s[q] = 0.5 * (1.0 + t) + 0.5 * v * (1.0 - t * t) * SLOPE * (
            1.0 + 3.0 * 0.044715 * v * v
        )

    def gh_part(q):
        spread(1, q, summed(1, q) * slope_s[q])

    stores = []

    def store(src, dst):
        stores.append(pltpu.make_async_copy(src, dst, loc.at[4 + len(stores)]))
        stores[-1].start()

    def turn(src, dst):
        def body(n):
            dst[cols(n), :] = src[:, :, :, cols(n)].reshape(256, cw).astype(F32).T.astype(BF16)

        loop(body)

    def copy_a(w, part):
        return send(a_send.at[w, part], a_recv.at[w, part], la_s.at[w, part], la_r.at[w, part], sib)

    def copy_b(w):
        return send(b_send.at[w], b_recv.at[w], lb_s.at[w], lb_r.at[w], xnb)

    def copy_c(w, d):
        zz = (z + d) % 8
        return send(z_send.at[w, zz], z_recv.at[w, d], lc_s.at[w, d], lc_r.at[w, d], col_dev(zz, xl, k))

    def project(w, q, put):
        full = (a_all, g_all)[w]
        for i in range(7):
            gather_copy(w, q, i).wait_recv()

        def body(n):
            left = full[q].reshape(64, width)
            part = dot_nn(left, w2d[:, cols(n)]) if w == 0 else dot_nt(left, w1d[cols(n), :])
            put(n, part.reshape(8, 8, cw))

        loop(body)

    def to_sibling(w, part, q):
        def put(n, value):
            a_send[w, part, :, :, cols(n)] = value.astype(BF16)

        project(w, q, put)
        copy_a(w, part).start()

    def far_half(w):
        to_sibling(w, 0, 3)

        def put(n, value):
            own_there[:, :, cols(n)] = value

        project(w, 2, put)
        copy_a(w, 0).wait_recv()
        b_send[w] = (own_there[...] + a_recv[w, 0].astype(F32)).astype(BF16)
        copy_b(w).start()

    def near_half(w):
        to_sibling(w, 1, 1)

        def put(n, value):
            own_here[w, :, :, cols(n)] = value

        project(w, 0, put)

    def over_z(w):
        copy_a(w, 1).wait_recv()
        copy_b(w).wait_recv()
        total = own_here[w] + a_recv[w, 1].astype(F32) + b_recv[w].astype(F32)
        own_here[w] = total
        z_send[w] = total.astype(BF16)
        for d in Z_ORDER:
            copy_c(w, d).start()

    def last(w):
        total = own_here[w, z]
        for d in Z_WAIT:
            copy_c(w, d).wait_recv()
        for d in range(1, 8):
            total = total + z_recv[w, d].astype(F32)
        (out_o, tg_o)[w][...] = total.astype(BF16)

    forward_z(0)
    scatter(0, (0,))
    forward_x(0)
    arrived(0, 0)
    scatter(0, (1,))
    scatter(0, (2,))
    forward_z(1)
    arrived(0, 8)
    scatter(0, (3,))
    forward_x(1)
    arrived(1, 0)
    scatter(1, (0, 1))
    arrived(1, 8)
    scatter(1, (2, 3))
    turn(t_all, t_turn)
    store(t_turn, t_o)
    store(c_all, c_o)
    for q in (3, 2, 1, 0):
        act_part(q)
    for q in (3, 2, 1, 0):
        gh_part(q)
    far_half(0)
    near_half(0)
    turn(a_all, a_turn)
    store(a_turn, a_o)
    far_half(1)
    over_z(0)
    near_half(1)
    over_z(1)
    store(g_all, g_o)
    last(0)
    last(1)

    for table in (zc, xc, bc):
        for copy in table.values():
            copy.wait_send()
    for w in range(2):
        for q in range(4):
            for i in range(7):
                scatter_copy(w, q, i).wait_send()
                gather_copy(w, q, i).wait_send()
        copy_a(w, 0).wait_send()
        copy_a(w, 1).wait_send()
        copy_b(w).wait_send()
        for d in range(1, 8):
            copy_c(w, d).wait_send()
    for s in stores:
        s.wait()


def block_grads(
    m1, m2, t_h, c_h, a_h, g_h, out_i, tg_i, g1_o, g2_o, out_o, tg_o, bg_o,
    t, c, a, g, b1, b2, i1, i2, sems, puts,
):
    width = c.shape[-1]
    groups = b1.shape[0] // GROUP
    loads = [
        pltpu.make_async_copy(src, dst, sems.at[i])
        for i, (src, dst) in enumerate(((g_h, g), (t_h, t), (a_h, a), (c_h, c)))
    ]
    for load in loads:
        load.start()
    out_o[...] = out_i[...]
    tg_o[...] = tg_i[...]
    counts = []
    for mask, table in ((m1, i1), (m2, i2)):
        tr, tc = mask.shape

        def one_row(i, slot):
            for j in range(tc):
                table[slot] = i * tc + j
                slot = slot + mask[i, j]
            return slot

        counts.append(lax.fori_loop(0, tr, one_row, jnp.int32(0)))

    def tall(ref, i):
        return ref[pl.ds(pl.multiple_of(i * BLK, BLK), BLK), :]

    def wide(ref, i):
        return ref[:, :, :, pl.ds(pl.multiple_of(i * BLK, BLK), BLK)].reshape(256, BLK)

    def put(which, at):
        src, dst = ((b1, g1_o), (b2, g2_o))[which]
        part = pl.ds(at * GROUP, GROUP)
        return pltpu.make_async_copy(src.at[part], dst.at[part], puts.at[which, at])

    for which, (left, right, mask, table, dest) in enumerate(((t, g, m1, i1, b1), (a, c, m2, i2, b2))):
        tc = mask.shape[1]
        loads[2 * which].wait()
        loads[2 * which + 1].wait()

        def one_group(at, carry):
            for u in range(GROUP):
                slot = at * GROUP + u
                live = slot < counts[which]
                place = jnp.where(live, table[slot], 0)
                grad = dot_nn(tall(left, place // tc), wide(right, place % tc))
                dest[slot] = jnp.where(live, grad, 0.0)
            put(which, at).start()
            return carry

        lax.fori_loop(0, groups, one_group, 0)
    bg_o[...] = jnp.sum(g[...].reshape(256, width).astype(F32), axis=0)
    for which in range(2):
        lax.fori_loop(0, groups, lambda at, x: (put(which, at).wait(), x)[1], 0)


def local(tokens, cotangent, w1_mask, w1_blocks, bias, w2_mask, w2_blocks):
    rows, width = tokens.shape
    total = 256
    cap = w1_blocks.shape[2]
    w1b = w1_blocks.reshape(w1_blocks.shape[2:])
    w2b = w2_blocks.reshape(w2_blocks.shape[2:])
    vmem = pl.BlockSpec(memory_space=pltpu.VMEM)
    smem = pl.BlockSpec(memory_space=pltpu.SMEM)
    anyw = pl.BlockSpec(memory_space=pl.ANY)
    small = jax.ShapeDtypeStruct((rows, width), BF16)
    turned = jax.ShapeDtypeStruct((width, total), BF16)
    quarters = (4, 8, rows, width)
    full = jax.ShapeDtypeStruct(quarters, BF16)
    dma = pltpu.SemaphoreType.DMA
    V = pltpu.VMEM
    params = dict(vmem_limit_bytes=67043328)
    out, tg, t, c, a, g = pl.pallas_call(
        mega,
        name="mega",
        out_shape=(small, small, turned, full, turned, full),
        in_specs=[vmem, vmem, smem, smem, vmem, anyw, anyw],
        out_specs=(vmem, vmem, anyw, anyw, anyw, anyw),
        scratch_shapes=[
            V(quarters, BF16), V(quarters, BF16), V(quarters, BF16), V(quarters, BF16),
            V((width, width), BF16), V((width, width), BF16),
            V((cap, BLK, BLK), BF16), V((cap, BLK, BLK), BF16),
            V(quarters, BF16), V(quarters, BF16),
            V((4, 7, rows, width), BF16), V((4, 7, rows, width), BF16),
            V((4, rows, width), F32), V((1, width), F32),
            V((2, 2, 8, rows, width), BF16), V((2, 2, 8, rows, width), BF16),
            V((8, rows, width), F32), V((2, 8, rows, width), F32),
            V((2, 8, rows, width), BF16), V((2, 8, rows, width), BF16),
            V((2, 8, rows, width), BF16), V((2, 8, rows, width), BF16),
            V((width, total), BF16), V((width, total), BF16),
            dma((8,)), dma((2, 8)), dma((2, 8)), dma((2, 8)), dma((2, 8)), dma((2, 16)), dma((2, 16)),
            dma((2, 4, 7)), dma((2, 4, 7)), dma((2, 4, 7)), dma((2, 4, 7)),
            dma((2, 2)), dma((2, 2)), dma((2,)), dma((2,)), dma((2, 8)), dma((2, 8)),
        ],
        compiler_params=pltpu.CompilerParams(collective_id=0, has_side_effects=True, **params),
    )(tokens, cotangent, w1_mask, w2_mask, bias, w1b, w2b)

    grads = jax.ShapeDtypeStruct((cap, BLK, BLK), F32)
    g1, g2, out, tg, bg = pl.pallas_call(
        block_grads,
        name="block_grads",
        out_shape=(grads, grads, small, small, jax.ShapeDtypeStruct((width,), F32)),
        in_specs=[smem, smem] + [anyw] * 4 + [vmem] * 2,
        out_specs=(anyw, anyw, vmem, vmem, vmem),
        scratch_shapes=[
            V((width, total), BF16), V(quarters, BF16), V((width, total), BF16), V(quarters, BF16),
            V((cap, BLK, BLK), F32), V((cap, BLK, BLK), F32),
            pltpu.SMEM((cap + 8,), jnp.int32), pltpu.SMEM((cap + 8,), jnp.int32),
            dma((4,)), dma((2, cap // GROUP)),
        ],
        compiler_params=pltpu.CompilerParams(**params),
    )(w1_mask, w2_mask, t, c, a, g, out, tg)
    return out, tg, g1[None, None], g2[None, None], bg


def solution(mesh):
    weights = P("row", "col", None, None, None)
    return jax.shard_map(
        local,
        mesh=mesh,
        in_specs=(P("col", "row"), P("col", "row"), P("row", "col"), weights, P("col"), P("col", "row"), weights),
        out_specs=(P("col", "row"), P("col", "row"), weights, weights, P("col")),
        check_vma=False,
    )
```

time: 90.1 us -> 92.5 us (1.027); the launches traced: 88.5 us -> 92.3 us
  Pallas kernels: 87.9 us -> 91.6 us
    pallas_call x2, Pallas kernels: 87.9 us -> 91.6 us  [the longest x1 82.1 us: local(): pl.pallas_call(mega, name='mega', out_shape=(small, small, turned, full,...]
where the time goes in v3:
time: 92.5 us; the launch traced here: 92.3 us
  Pallas kernels  91.6 us (99%)
    pallas_call x1, Pallas kernels, local(): pl.pallas_call(mega, name='mega', out_shape=(small, small, turned, full,...  82.1 us
    pallas_call x1, Pallas kernels, local(): pl.pallas_call(block_grads, name='block_grads', out_shape=(grads, grads,...  9.51 us

profile of v3, /device:TPU:1, one launch (start us, length us, event | category | flops | bytes accessed | tf_op | source)
XLA Modules:
  0.0 92.3 jit_solution(16404578770952408117)
XLA Ops:
  0.6 82.1 %mega.1 = (bf16[8,1536]{1,0:T(8,128)(2,1)}, bf16[8,1536]{1,0:T(8,128)(2,1)}, bf16[1536,256]{1,0:T(8,128)(2,1)}, bf16[4,8,8,1536]{3,2,1,0:T(8,128)(2,1)}, bf16[15...) custom-call(bf16[8,1536]{1,0:T(8,128)(2,1)} %tok.1, bf16[8,1536]{1,0:T(8,128)(2,1)} %cot.1, s32[12,12]{1,0:T(8,128)} %m1.3, ...), custom_call_target="tpu_custom_call" | custom-call | tf_op jit(solution)/shard_map/mega/pallas_call | solution.py:388
  82.8 9.5 %block_grads.1 = (f32[48,128,128]{2,1,0:T(8,128)}, f32[48,128,128]{2,1,0:T(8,128)}, bf16[8,1536]{1,0:T(8,128)(2,1)}, bf16[8,1536]{1,0:T(8,128)(2,1)}, f32[1536]{0:T(1024)}) custom-call(s32[12,12]{1,0:T(8,128)} %m1.3, s32[12,12]{1,0:T(8,128)} %m2.3, bf16[1536,256]{1,0:T(8,128)(2,1)} %get-tuple-element.16.t_h, bf16[4,8,8,1536]{3,2,1,0:T(8,128)(2,1)} %get-tuple-element.17.c_h, ...), custom_call_target="tpu_custom_call" | custom-call | tf_op jit(solution)/shard_map/block_grads/pallas_call | solution.py:414

commit v4 on v3

--- a/solution.py
+++ b/solution.py
@@ -10,14 +10,14 @@
 
 MESH = pl.DeviceIdType.MESH
 BLK = 128
-GROUP = 4
+GROUP = 8
 NCH = 3
 F32 = jnp.float32
 BF16 = jnp.bfloat16
 SLOPE = math.sqrt(2.0 / math.pi)
 Z_ORDER = (4, 3, 5, 2, 6, 1, 7)
 Z_WAIT = (1, 7, 2, 6, 3, 5, 4)
-ROW_ORDER = ((2, 1), (1, 1), (3, 1), (0, 1), (2, 0), (1, 0), (3, 0))
+Y_ORDER = (2, 1, 3)
 
 
 def dot_nn(a, b):
@@ -32,9 +32,9 @@
     tok, cot, m1, m2, bias, w1, w2,
     out_o, tg_o, t_o, c_o, a_o, g_o,
     t_all, c_all, a_all, g_all, w1d, w2d, wb1, wb2,
-    h_send, ga_send, h_recv, ga_recv, slope_s, bias_s,
+    h_send, ga_send, h_recv, ga_recv, f_send, f_recv, slope_s, bias_s,
     a_send, a_recv, own_there, own_here, b_send, b_recv, z_send, z_recv, t_turn, a_turn,
-    loc, zs, zr, xs, xr, bs, br, rs_s, rs_r, ag_s, ag_r, la_s, la_r, lb_s, lb_r, lc_s, lc_r,
+    loc, zs, zr, xs, xr, bs, br, rs_s, rs_r, fo_s, fo_r, ag_s, ag_r, la_s, la_r, lb_s, lb_r, lc_s, lc_r,
 ):
     width = tok.shape[1]
     cw = width // NCH
@@ -58,7 +58,9 @@
 
     sib = col_dev(z, xl, 1 - k)
     xnb = col_dev(z, 1 - xl, k)
-    peers = [row_dev(dy, dx) for dy, dx in ROW_ORDER]
+    partner = row_dev(0, 1)
+    other = y * 2 + 1 - xh
+    peers = [row_dev(d, 0) for d in Y_ORDER] + [partner]
     peers += [col_dev((z + d) % 8, xl, k) for d in range(1, 8)] + [sib, xnb]
 
     load1 = pltpu.make_async_copy(w1, wb1, loc.at[0])
@@ -138,12 +140,17 @@
 
     def scatter_copy(w, q, i):
         buf, got = ((h_send, h_recv), (ga_send, ga_recv))[w]
-        dev = row_dev(*ROW_ORDER[i])
-        return send(buf.at[q, dev[0]], got.at[q, i], rs_s.at[w, q, i], rs_r.at[w, q, i], dev)
+        dev = row_dev(Y_ORDER[i % 3], 0)
+        share = dev[0] if i >= 3 else dev[0] + 1 - 2 * xh
+        return send(buf.at[q, share], got.at[q, i], rs_s.at[w, q, i], rs_r.at[w, q, i], dev)
+
+    def fold_copy(w, q):
+        return send(f_send.at[w, q], f_recv.at[w, q], fo_s.at[w, q], fo_r.at[w, q], partner)
 
     def gather_copy(w, q, i):
-        ref = (a_all, g_all)[w].at[q, row]
-        return send(ref, ref, ag_s.at[w, q, i], ag_r.at[w, q, i], row_dev(*ROW_ORDER[i]))
+        ref = (a_all, g_all)[w].at[q, row if i < 4 else other]
+        dev = partner if i == 3 else row_dev(Y_ORDER[i % 4], 0)
+        return send(ref, ref, ag_s.at[w, q, i], ag_r.at[w, q, i], dev)
 
     def scatter(w, quarters):
         full, buf = ((t_all, h_send), (c_all, ga_send))[w]
@@ -156,21 +163,37 @@
 
         loop(body)
         for q in quarters:
-            for i in range(7):
+            for i in range(6):
                 scatter_copy(w, q, i).start()
+
+    def fold(w, q):
+        buf, got = ((h_send, h_recv), (ga_send, ga_recv))[w]
+        for i in range(3):
+            scatter_copy(w, q, i).wait_recv()
+        total = buf[q, other].astype(F32)
+        for i in range(3):
+            total = total + got[q, i].astype(F32)
+        f_send[w, q] = total.astype(BF16)
+        fold_copy(w, q).start()
 
     def summed(w, q):
         buf, got = ((h_send, h_recv), (ga_send, ga_recv))[w]
-        total = buf[q, row].astype(F32)
-        for i in range(7):
+        for i in range(3, 6):
             scatter_copy(w, q, i).wait_recv()
-        for i in range(7):
+        fold_copy(w, q).wait_recv()
+        total = buf[q, row].astype(F32) + f_recv[w, q].astype(F32)
+        for i in range(3, 6):
             total = total + got[q, i].astype(F32)
         return total
 
     def spread(w, q, value):
         (a_all, g_all)[w][q, row] = value.astype(BF16)
-        for i in range(7):
+        for i in (3, 0, 1, 2):
+            gather_copy(w, q, i).start()
+
+    def relay(w, q):
+        gather_copy(w, q, 3).wait_recv()
+        for i in (4, 5, 6):
             gather_copy(w, q, i).start()
 
     def act_part(q):
@@ -208,7 +231,7 @@
 
     def project(w, q, put):
         full = (a_all, g_all)[w]
-        for i in range(7):
+        for i in (0, 1, 2, 4, 5, 6):
             gather_copy(w, q, i).wait_recv()
 
         def body(n):
@@ -220,7 +243,7 @@
 
     def to_sibling(w, part, q):
         def put(n, value):
-            a_send[w, part, :, :, cols(n)] = value.astype(BF16)
+            a_send[w, part, :, :, cols(n)] = value
 
         project(w, q, put)
         copy_a(w, part).start()
@@ -233,7 +256,7 @@
 
         project(w, 2, put)
         copy_a(w, 0).wait_recv()
-        b_send[w] = (own_there[...] + a_recv[w, 0].astype(F32)).astype(BF16)
+        b_send[w] = (own_there[...] + a_recv[w, 0]).astype(BF16)
         copy_b(w).start()
 
     def near_half(w):
@@ -247,7 +270,7 @@
     def over_z(w):
         copy_a(w, 1).wait_recv()
         copy_b(w).wait_recv()
-        total = own_here[w] + a_recv[w, 1].astype(F32) + b_recv[w].astype(F32)
+        total = own_here[w] + a_recv[w, 1] + b_recv[w].astype(F32)
         own_here[w] = total
         z_send[w] = total.astype(BF16)
         for d in Z_ORDER:
@@ -273,15 +296,25 @@
     forward_x(1)
     arrived(1, 0)
     scatter(1, (0, 1))
+    fold(0, 0)
+    fold(0, 1)
     arrived(1, 8)
     scatter(1, (2, 3))
-    turn(t_all, t_turn)
-    store(t_turn, t_o)
-    store(c_all, c_o)
+    fold(0, 2)
+    fold(0, 3)
     for q in (3, 2, 1, 0):
         act_part(q)
     for q in (3, 2, 1, 0):
+        fold(1, q)
+    for q in (3, 2, 1, 0):
+        relay(0, q)
+    for q in (3, 2, 1, 0):
         gh_part(q)
+    store(c_all, c_o)
+    for q in (3, 2, 1, 0):
+        relay(1, q)
+    turn(t_all, t_turn)
+    store(t_turn, t_o)
     far_half(0)
     near_half(0)
     turn(a_all, a_turn)
@@ -289,8 +322,8 @@
     far_half(1)
     over_z(0)
     near_half(1)
+    store(g_all, g_o)
     over_z(1)
-    store(g_all, g_o)
     last(0)
     last(1)
 
@@ -299,8 +332,10 @@
             copy.wait_send()
     for w in range(2):
         for q in range(4):
+            for i in range(6):
+                scatter_copy(w, q, i).wait_send()
+            fold_copy(w, q).wait_send()
             for i in range(7):
-                scatter_copy(w, q, i).wait_send()
                 gather_copy(w, q, i).wait_send()
         copy_a(w, 0).wait_send()
         copy_a(w, 1).wait_send()
@@ -315,7 +350,6 @@
     m1, m2, t_h, c_h, a_h, g_h, out_i, tg_i, g1_o, g2_o, out_o, tg_o, bg_o,
     t, c, a, g, b1, b2, i1, i2, sems, puts,
 ):
-    width = c.shape[-1]
     groups = b1.shape[0] // GROUP
     loads = [
         pltpu.make_async_copy(src, dst, sems.at[i])
@@ -341,7 +375,7 @@
         return ref[pl.ds(pl.multiple_of(i * BLK, BLK), BLK), :]
 
     def wide(ref, i):
-        return ref[:, :, :, pl.ds(pl.multiple_of(i * BLK, BLK), BLK)].reshape(256, BLK)
+        return ref[:, pl.ds(pl.multiple_of(i * BLK, BLK), BLK)]
 
     def put(which, at):
         src, dst = ((b1, g1_o), (b2, g2_o))[which]
@@ -364,7 +398,7 @@
             return carry
 
         lax.fori_loop(0, groups, one_group, 0)
-    bg_o[...] = jnp.sum(g[...].reshape(256, width).astype(F32), axis=0)
+    bg_o[...] = jnp.sum(g[...].astype(F32), axis=0)
     for which in range(2):
         lax.fori_loop(0, groups, lambda at, x: (put(which, at).wait(), x)[1], 0)
 
@@ -396,15 +430,16 @@
             V((width, width), BF16), V((width, width), BF16),
             V((cap, BLK, BLK), BF16), V((cap, BLK, BLK), BF16),
             V(quarters, BF16), V(quarters, BF16),
-            V((4, 7, rows, width), BF16), V((4, 7, rows, width), BF16),
+            V((4, 6, rows, width), BF16), V((4, 6, rows, width), BF16),
+            V((2, 4, rows, width), BF16), V((2, 4, rows, width), BF16),
             V((4, rows, width), F32), V((1, width), F32),
-            V((2, 2, 8, rows, width), BF16), V((2, 2, 8, rows, width), BF16),
+            V((2, 2, 8, rows, width), F32), V((2, 2, 8, rows, width), F32),
             V((8, rows, width), F32), V((2, 8, rows, width), F32),
             V((2, 8, rows, width), BF16), V((2, 8, rows, width), BF16),
             V((2, 8, rows, width), BF16), V((2, 8, rows, width), BF16),
             V((width, total), BF16), V((width, total), BF16),
             dma((8,)), dma((2, 8)), dma((2, 8)), dma((2, 8)), dma((2, 8)), dma((2, 16)), dma((2, 16)),
-            dma((2, 4, 7)), dma((2, 4, 7)), dma((2, 4, 7)), dma((2, 4, 7)),
+            dma((2, 4, 6)), dma((2, 4, 6)), dma((2, 4)), dma((2, 4)), dma((2, 4, 7)), dma((2, 4, 7)),
             dma((2, 2)), dma((2, 2)), dma((2,)), dma((2,)), dma((2, 8)), dma((2, 8)),
         ],
         compiler_params=pltpu.CompilerParams(collective_id=0, has_side_effects=True, **params),
@@ -418,13 +453,13 @@
         in_specs=[smem, smem] + [anyw] * 4 + [vmem] * 2,
         out_specs=(anyw, anyw, vmem, vmem, vmem),
         scratch_shapes=[
-            V((width, total), BF16), V(quarters, BF16), V((width, total), BF16), V(quarters, BF16),
+            V((width, total), BF16), V((total, width), BF16), V((width, total), BF16), V((total, width), BF16),
             V((cap, BLK, BLK), F32), V((cap, BLK, BLK), F32),
             pltpu.SMEM((cap + 8,), jnp.int32), pltpu.SMEM((cap + 8,), jnp.int32),
             dma((4,)), dma((2, cap // GROUP)),
         ],
         compiler_params=pltpu.CompilerParams(**params),
-    )(w1_mask, w2_mask, t, c, a, g, out, tg)
+    )(w1_mask, w2_mask, t, c.reshape(total, width), a, g.reshape(total, width), out, tg)
     return out, tg, g1[None, None], g2[None, None], bg
 
 

time: 92.5 us -> 84.4 us (0.912)
  Pallas kernels: 91.6 us -> 83.5 us
    pallas_call x1, Pallas kernels: 82.1 us -> 75.9 us  [local(): pl.pallas_call(mega, name='mega', out_shape=(small, small, turned, full,...]
    pallas_call x1, Pallas kernels: 9.51 us -> 7.63 us  [local(): pl.pallas_call(block_grads, name='block_grads', out_shape=(grads, grads,...]
where the time goes in v4:
time: 84.4 us; the launch traced here: 84.1 us
  Pallas kernels  83.5 us (99%)
    pallas_call x1, Pallas kernels, local(): pl.pallas_call(mega, name='mega', out_shape=(small, small, turned, full,...  75.9 us
    pallas_call x1, Pallas kernels, local(): pl.pallas_call(block_grads, name='block_grads', out_shape=(grads, grads,...  7.63 us

profile of v4, /device:TPU:1, one launch (start us, length us, event | category | flops | bytes accessed | tf_op | source)
XLA Modules:
  0.0 84.1 jit_solution(7119780113931811550)
XLA Ops:
  0.6 75.9 %mega.1 = (bf16[8,1536]{1,0:T(8,128)(2,1)}, bf16[8,1536]{1,0:T(8,128)(2,1)}, bf16[1536,256]{1,0:T(8,128)(2,1)}, bf16[4,8,8,1536]{3,2,1,0:T(8,128)(2,1)}, bf16[15...) custom-call(bf16[8,1536]{1,0:T(8,128)(2,1)} %tok.1, bf16[8,1536]{1,0:T(8,128)(2,1)} %cot.1, s32[12,12]{1,0:T(8,128)} %m1.3, ...), custom_call_target="tpu_custom_call" | custom-call | tf_op jit(solution)/shard_map/mega/pallas_call | solution.py:422
  76.5 7.6 %block_grads.1 = (f32[48,128,128]{2,1,0:T(8,128)}, f32[48,128,128]{2,1,0:T(8,128)}, bf16[8,1536]{1,0:T(8,128)(2,1)}, bf16[8,1536]{1,0:T(8,128)(2,1)}, f32[1536]{0:T(1024)}) custom-call(s32[12,12]{1,0:T(8,128)} %m1.3, s32[12,12]{1,0:T(8,128)} %m2.3, bf16[1536,256]{1,0:T(8,128)(2,1)} %get-tuple-element.16.t_h, bf16[256,1536]{1,0:T(8,128)(2,1)} %bitcast.8, ...), custom_call_target="tpu_custom_call" | custom-call | tf_op jit(solution)/shard_map/block_grads/pallas_call | solution.py:449

commit v5 on v4

--- a/solution.py
+++ b/solution.py
@@ -38,6 +38,7 @@
 ):
     width = tok.shape[1]
     cw = width // NCH
+    sides = (slice(0, width // 2), slice(width // 2, width))
     row, col = lax.axis_index("row"), lax.axis_index("col")
     y, xh = row // 2, row % 2
     z, xl, k = col // 4, (col // 2) % 2, col % 2
@@ -222,12 +223,14 @@
     def copy_a(w, part):
         return send(a_send.at[w, part], a_recv.at[w, part], la_s.at[w, part], la_r.at[w, part], sib)
 
-    def copy_b(w):
-        return send(b_send.at[w], b_recv.at[w], lb_s.at[w], lb_r.at[w], xnb)
-
-    def copy_c(w, d):
+    def copy_b(w, h):
+        return send(b_send.at[w, h], b_recv.at[w, h], lb_s.at[w, h], lb_r.at[w, h], xnb)
+
+    def copy_c(w, h, d):
         zz = (z + d) % 8
-        return send(z_send.at[w, zz], z_recv.at[w, d], lc_s.at[w, d], lc_r.at[w, d], col_dev(zz, xl, k))
+        return send(
+            z_send.at[w, h, zz], z_recv.at[w, h, d], lc_s.at[w, h, d], lc_r.at[w, h, d], col_dev(zz, xl, k)
+        )
 
     def project(w, q, put):
         full = (a_all, g_all)[w]
@@ -256,8 +259,9 @@
 
         project(w, 2, put)
         copy_a(w, 0).wait_recv()
-        b_send[w] = (own_there[...] + a_recv[w, 0]).astype(BF16)
-        copy_b(w).start()
+        for h, side in enumerate(sides):
+            b_send[w, h] = (own_there[:, :, side] + a_recv[w, 0, :, :, side]).astype(BF16)
+            copy_b(w, h).start()
 
     def near_half(w):
         to_sibling(w, 1, 1)
@@ -269,52 +273,59 @@
 
     def over_z(w):
         copy_a(w, 1).wait_recv()
-        copy_b(w).wait_recv()
-        total = own_here[w] + a_recv[w, 1] + b_recv[w].astype(F32)
-        own_here[w] = total
-        z_send[w] = total.astype(BF16)
-        for d in Z_ORDER:
-            copy_c(w, d).start()
+        for h, side in enumerate(sides):
+            copy_b(w, h).wait_recv()
+            total = own_here[w, :, :, side] + a_recv[w, 1, :, :, side] + b_recv[w, h].astype(F32)
+            own_here[w, :, :, side] = total
+            z_send[w, h] = total.astype(BF16)
+            for d in Z_ORDER:
+                copy_c(w, h, d).start()
 
     def last(w):
-        total = own_here[w, z]
-        for d in Z_WAIT:
-            copy_c(w, d).wait_recv()
-        for d in range(1, 8):
-            total = total + z_recv[w, d].astype(F32)
-        (out_o, tg_o)[w][...] = total.astype(BF16)
+        for h, side in enumerate(sides):
+            total = own_here[w, z, :, side]
+            for d in Z_WAIT:
+                copy_c(w, h, d).wait_recv()
+            for d in range(1, 8):
+                total = total + z_recv[w, h, d].astype(F32)
+            (out_o, tg_o)[w][:, side] = total.astype(BF16)
 
     forward_z(0)
     scatter(0, (0,))
+    forward_z(1)
     forward_x(0)
     arrived(0, 0)
     scatter(0, (1,))
-    scatter(0, (2,))
-    forward_z(1)
     arrived(0, 8)
-    scatter(0, (3,))
+    scatter(0, (2, 3))
     forward_x(1)
+    fold(0, 0)
+    fold(0, 1)
     arrived(1, 0)
     scatter(1, (0, 1))
-    fold(0, 0)
-    fold(0, 1)
+    fold(0, 2)
+    fold(0, 3)
     arrived(1, 8)
     scatter(1, (2, 3))
-    fold(0, 2)
-    fold(0, 3)
     for q in (3, 2, 1, 0):
         act_part(q)
-    for q in (3, 2, 1, 0):
+    turn(t_all, t_turn)
+    store(t_turn, t_o)
+    store(c_all, c_o)
+    for q in (3, 2):
+        relay(0, q)
+    for q in (3, 2):
         fold(1, q)
-    for q in (3, 2, 1, 0):
+    for q in (1, 0):
         relay(0, q)
-    for q in (3, 2, 1, 0):
+    for q in (1, 0):
+        fold(1, q)
+    for q in (3, 2):
         gh_part(q)
-    store(c_all, c_o)
+    for q in (1, 0):
+        gh_part(q)
     for q in (3, 2, 1, 0):
         relay(1, q)
-    turn(t_all, t_turn)
-    store(t_turn, t_o)
     far_half(0)
     near_half(0)
     turn(a_all, a_turn)
@@ -339,9 +350,10 @@
                 gather_copy(w, q, i).wait_send()
         copy_a(w, 0).wait_send()
         copy_a(w, 1).wait_send()
-        copy_b(w).wait_send()
-        for d in range(1, 8):
-            copy_c(w, d).wait_send()
+        for h in range(2):
+            copy_b(w, h).wait_send()
+            for d in range(1, 8):
+                copy_c(w, h, d).wait_send()
     for s in stores:
         s.wait()
 
@@ -435,12 +447,12 @@
             V((4, rows, width), F32), V((1, width), F32),
             V((2, 2, 8, rows, width), F32), V((2, 2, 8, rows, width), F32),
             V((8, rows, width), F32), V((2, 8, rows, width), F32),
-            V((2, 8, rows, width), BF16), V((2, 8, rows, width), BF16),
-            V((2, 8, rows, width), BF16), V((2, 8, rows, width), BF16),
+            V((2, 2, 8, rows, width // 2), BF16), V((2, 2, 8, rows, width // 2), BF16),
+            V((2, 2, 8, rows, width // 2), BF16), V((2, 2, 8, rows, width // 2), BF16),
             V((width, total), BF16), V((width, total), BF16),
             dma((8,)), dma((2, 8)), dma((2, 8)), dma((2, 8)), dma((2, 8)), dma((2, 16)), dma((2, 16)),
             dma((2, 4, 6)), dma((2, 4, 6)), dma((2, 4)), dma((2, 4)), dma((2, 4, 7)), dma((2, 4, 7)),
-            dma((2, 2)), dma((2, 2)), dma((2,)), dma((2,)), dma((2, 8)), dma((2, 8)),
+            dma((2, 2)), dma((2, 2)), dma((2, 2)), dma((2, 2)), dma((2, 2, 8)), dma((2, 2, 8)),
         ],
         compiler_params=pltpu.CompilerParams(collective_id=0, has_side_effects=True, **params),
     )(tokens, cotangent, w1_mask, w2_mask, bias, w1b, w2b)

time: 84.4 us -> 84.1 us (level)
  no operation moved by 1% of the time
where the time goes in v5:
time: 84.1 us; the launch traced here: 83.5 us
  Pallas kernels  82.9 us (99%)
    pallas_call x1, Pallas kernels, local(): pl.pallas_call(mega, name='mega', out_shape=(small, small, turned, full,...  75.3 us
    pallas_call x1, Pallas kernels, local(): pl.pallas_call(block_grads, name='block_grads', out_shape=(grads, grads,...  7.63 us

profile of v5, /device:TPU:1, one launch (start us, length us, event | category | flops | bytes accessed | tf_op | source)
XLA Modules:
  0.0 83.5 jit_solution(15880928771301936938)
XLA Ops:
  0.6 75.3 %mega.1 = (bf16[8,1536]{1,0:T(8,128)(2,1)}, bf16[8,1536]{1,0:T(8,128)(2,1)}, bf16[1536,256]{1,0:T(8,128)(2,1)}, bf16[4,8,8,1536]{3,2,1,0:T(8,128)(2,1)}, bf16[15...) custom-call(bf16[8,1536]{1,0:T(8,128)(2,1)} %tok.1, bf16[8,1536]{1,0:T(8,128)(2,1)} %cot.1, s32[12,12]{1,0:T(8,128)} %m1.3, ...), custom_call_target="tpu_custom_call" | custom-call | tf_op jit(solution)/shard_map/mega/pallas_call | solution.py:434
  75.9 7.6 %block_grads.1 = (f32[48,128,128]{2,1,0:T(8,128)}, f32[48,128,128]{2,1,0:T(8,128)}, bf16[8,1536]{1,0:T(8,128)(2,1)}, bf16[8,1536]{1,0:T(8,128)(2,1)}, f32[1536]{0:T(1024)}) custom-call(s32[12,12]{1,0:T(8,128)} %m1.3, s32[12,12]{1,0:T(8,128)} %m2.3, bf16[1536,256]{1,0:T(8,128)(2,1)} %get-tuple-element.16.t_h, bf16[256,1536]{1,0:T(8,128)(2,1)} %bitcast.8, ...), custom_call_target="tpu_custom_call" | custom-call | tf_op jit(solution)/shard_map/block_grads/pallas_call | solution.py:461

commit v6 on v5

--- a/solution.py
+++ b/solution.py
@@ -10,7 +10,7 @@
 
 MESH = pl.DeviceIdType.MESH
 BLK = 128
-GROUP = 8
+GROUP = 16
 NCH = 3
 F32 = jnp.float32
 BF16 = jnp.bfloat16

time: 84.1 us -> 83.2 us (0.989)
  Pallas kernels: 82.9 us -> 82 us
    pallas_call x1, Pallas kernels: 7.63 us -> 6.72 us  [local(): pl.pallas_call(block_grads, name='block_grads', out_shape=(grads, grads,...]
where the time goes in v6:
time: 83.2 us; the launch traced here: 82.6 us
  Pallas kernels  82 us (99%)
    pallas_call x1, Pallas kernels, local(): pl.pallas_call(mega, name='mega', out_shape=(small, small, turned, full,...  75.3 us
    pallas_call x1, Pallas kernels, local(): pl.pallas_call(block_grads, name='block_grads', out_shape=(grads, grads,...  6.72 us

profile of v6, /device:TPU:1, one launch (start us, length us, event | category | flops | bytes accessed | tf_op | source)
XLA Modules:
  0.0 82.6 jit_solution(17177667923712898187)
XLA Ops:
  0.6 75.3 %mega.1 = (bf16[8,1536]{1,0:T(8,128)(2,1)}, bf16[8,1536]{1,0:T(8,128)(2,1)}, bf16[1536,256]{1,0:T(8,128)(2,1)}, bf16[4,8,8,1536]{3,2,1,0:T(8,128)(2,1)}, bf16[15...) custom-call(bf16[8,1536]{1,0:T(8,128)(2,1)} %tok.1, bf16[8,1536]{1,0:T(8,128)(2,1)} %cot.1, s32[12,12]{1,0:T(8,128)} %m1.3, ...), custom_call_target="tpu_custom_call" | custom-call | tf_op jit(solution)/shard_map/mega/pallas_call | solution.py:434
  75.9 6.7 %block_grads.1 = (f32[48,128,128]{2,1,0:T(8,128)}, f32[48,128,128]{2,1,0:T(8,128)}, bf16[8,1536]{1,0:T(8,128)(2,1)}, bf16[8,1536]{1,0:T(8,128)(2,1)}, f32[1536]{0:T(1024)}) custom-call(s32[12,12]{1,0:T(8,128)} %m1.3, s32[12,12]{1,0:T(8,128)} %m2.3, bf16[1536,256]{1,0:T(8,128)(2,1)} %get-tuple-element.16.t_h, bf16[256,1536]{1,0:T(8,128)(2,1)} %bitcast.8, ...), custom_call_target="tpu_custom_call" | custom-call | tf_op jit(solution)/shard_map/block_grads/pallas_call | solution.py:461
